TPU v7x, 768 devices: a whole 4x8x12 slice. The times are simulated.
768 devices in a mesh: dp: 48 (over y_lo, z, core), section: 4 (over y_hi), mp: 4 (over x).
Axes of the slice: x: 4, y: 8 (y_hi: 4, y_lo: 2; y = y_hi * 2 + y_lo), z: 12, core: 2. Of those that a mesh axis runs over, the one named last changes fastest.
Arguments:
- feature_bank: bfloat16 [12288, 1152], P('dp'), may hold values from -6 to 6
- feature_scale: float32 [48, 9], P('dp'), may hold values from 0.25 to 4
- shard_owner: int32 [48], replicated, may hold values from 0 to 47, each once
- image_shard: int32 [6144, 1], P('dp'), may hold values from 0 to 47; in each aligned block of 128 rows (0 to 127, 128 to 255, ...) at most 5 rows name the same one
- image_row: int32 [6144], P('dp'), may hold values from 0 to 255
- text_doc: int32 [48, 1024], P('dp'), may hold values from 0 to 7, never falling along the last dimension, each value on 1 to 512 neighbouring positions
- image_count: int32 [48, 8], P('dp'), may hold values from 1 to 64, 128 in all within a row
- proj_weight: bfloat16 [1152, 8192], P(None, ('section', 'mp')), may hold values from -0.1875 to 0.1875
- kv_weight: bfloat16 [32768, 1024], P('section', 'mp'), may hold values from -0.0625 to 0.0625
- queries: bfloat16 [49152, 16384], P('dp', ('section', 'mp')), may hold values from -48 to 48
- out_grad: bfloat16 [49152, 16384], P('dp', ('section', 'mp')), may hold values from -0.375 to 0.375
Outputs:
- proj_grad: float32 [1152, 8192], P('dp', ('section', 'mp'))
Inputs may be any that keep to these rules, and one draw needn't show every extreme that they name: `image_shard`: the 128 image tokens of one data group name no shard more than 5 times. `shard_owner`: each dp index once. `text_doc`: never falls along a sequence; each of the 8 documents has at least one token. `image_count`: the 8 counts of a data group sum to 128.
All inputs are finite; a program needn't handle non-finite values.
Results may differ from a plain program's by a relative error of at most 0.0085.
Values may be sent and summed in bfloat16 or wider, within the bound.
A program may use at most 64 MiB of HBM per device.

v0:
```python
import jax
import jax.numpy as jnp
from jax import lax
from jax.sharding import PartitionSpec as P

QBLK = 128


def joined_along(tiles, dim):
    tiles = jnp.moveaxis(tiles, 0, dim)
    dims = tiles.shape
    return tiles.reshape(*dims[:dim], dims[dim] * dims[dim + 1], *dims[dim + 2 :])


def copy_for_each(array, axis):
    peers = lax.axis_size(axis)
    return lax.all_to_all(
        jnp.broadcast_to(array[None], (peers, *array.shape)), axis, 0, 0, tiled=True
    )


def gathered_copies(array, axis, dim):
    return joined_along(copy_for_each(array, axis), dim)


def split_up(array, dim, peers):
    dims = array.shape
    tiles = array.reshape(*dims[:dim], peers, dims[dim] // peers, *dims[dim + 1 :])
    return jnp.moveaxis(tiles, dim, 0)


def sum_at_owner(array, axis, dim):
    peers = lax.axis_size(axis)
    tiles = lax.all_to_all(split_up(array, dim, peers), axis, 0, 0, tiled=True)
    return jnp.sum(tiles, axis=0)


def gelu(values):
    inner = 0.7978845608028654 * (values + 0.044715 * values * values * values)
    return 0.5 * values * (1.0 + jnp.tanh(inner))


def gelu_slope(values):
    inner = 0.7978845608028654 * (values + 0.044715 * values * values * values)
    tangent = jnp.tanh(inner)
    return 0.5 * (1.0 + tangent) + 0.5 * values * (1.0 - tangent * tangent) * 0.7978845608028654 * (
        1.0 + 3.0 * 0.044715 * values * values
    )


def head_backward(query_heads, grad_heads, key_value, token_doc, image_doc):
    head_size = key_value.shape[-1] // 2
    key_raw = key_value[:, :head_size]
    values_low = key_value[:, head_size:].astype(jnp.bfloat16)
    inv_norm = lax.rsqrt(jnp.mean(key_raw * key_raw, axis=-1, keepdims=True) + 1e-06)
    key_unit = key_raw * inv_norm
    key_low = key_unit.astype(jnp.bfloat16)
    score_scale = head_size ** (-0.5)
    scores = (
        jnp.einsum("tgd,id->gti", query_heads, key_low, preferred_element_type=jnp.float32)
        * score_scale
    )
    same_doc = (token_doc[:, None] == image_doc[None, :])[None, :, :]
    scores = jnp.where(same_doc, scores, -1e30)
    row_max = jnp.max(scores, axis=-1, keepdims=True)
    raised = jnp.where(same_doc, jnp.exp(scores - row_max), 0.0)
    probs = raised / jnp.sum(raised, axis=-1, keepdims=True)
    probs_low = probs.astype(jnp.bfloat16)
    dprobs = jnp.einsum("tgd,id->gti", grad_heads, values_low, preferred_element_type=jnp.float32)
    dscores = probs * (dprobs - jnp.sum(probs * dprobs, axis=-1, keepdims=True))
    dscores_low = dscores.astype(jnp.bfloat16)
    dvalues = jnp.einsum("gti,tgd->id", probs_low, grad_heads, preferred_element_type=jnp.float32)
    key_grad = (
        jnp.einsum("gti,tgd->id", dscores_low, query_heads, preferred_element_type=jnp.float32)
        * score_scale
    )
    raw_grad = inv_norm * (
        key_grad - key_unit * jnp.mean(key_grad * key_unit, axis=-1, keepdims=True)
    )
    return jnp.concatenate([raw_grad, dvalues], axis=-1).astype(jnp.bfloat16)


def body(
    feature_bank,
    feature_scale,
    shard_owner,
    image_shard,
    image_row,
    text_doc,
    image_count,
    proj_weight,
    kv_weight,
    queries,
    out_grad,
):
    groups = lax.axis_size("dp")
    images = image_row.shape[0]
    capacity = max(2, 2 * images // groups)
    owner_dev = shard_owner[image_shard[:, 0]]
    chosen = (owner_dev[:, None] == jnp.arange(groups, dtype=jnp.int32)[None, :]).astype(jnp.int32)
    earlier = jnp.cumsum(chosen, axis=0) - chosen
    slot_index = jnp.sum(earlier * chosen, axis=1)
    wanted = (
        jnp.zeros((groups * capacity,), jnp.int32)
        .at[owner_dev * capacity + slot_index]
        .set(image_row)
    )
    wanted = wanted.reshape(groups, capacity)
    columns = jnp.repeat(feature_scale[0], QBLK)
    slice_width = feature_bank.shape[1] // lax.axis_size(("section", "mp"))
    first_column = lax.axis_index(("section", "mp")) * slice_width
    stored = lax.dynamic_slice_in_dim(feature_bank, first_column, slice_width, 1)
    factors = lax.dynamic_slice_in_dim(columns, first_column, slice_width, 0)
    looked = stored[lax.all_to_all(wanted, "dp", split_axis=0, concat_axis=0, tiled=True)]
    scaled = (looked.astype(jnp.float32) * factors).astype(jnp.bfloat16)
    arrived = lax.all_to_all(scaled, "dp", split_axis=0, concat_axis=0, tiled=True)
    features = arrived[owner_dev, slot_index]
    features = gathered_copies(features, ("section", "mp"), 1)
    pre_act = jnp.dot(features, proj_weight, preferred_element_type=jnp.float32)
    embedded = gelu(pre_act).astype(jnp.bfloat16)
    key_value = jnp.dot(
        gathered_copies(embedded, ("section", "mp"), 1),
        kv_weight,
        preferred_element_type=jnp.float32,
    )
    doc_ends = jnp.cumsum(image_count[0])
    positions = jnp.arange(images, dtype=jnp.int32)
    image_doc = jnp.sum((doc_ends[None, :] <= positions[:, None]).astype(jnp.int32), axis=1)
    head_size = kv_weight.shape[1] // 2
    tokens = queries.shape[0]
    query_heads = queries.reshape(tokens, -1, head_size)
    grad_heads = out_grad.reshape(tokens, -1, head_size)
    kv_grad = head_backward(query_heads, grad_heads, key_value, text_doc[0], image_doc)
    proj_cols = proj_weight.shape[1]
    whole_grad = lax.dot_general(
        kv_weight, kv_grad, (((1,), (1,)), ((), ())), preferred_element_type=jnp.float32
    )
    whole_grad = whole_grad.reshape(
        lax.axis_size("section"), lax.axis_size("mp"), proj_cols, images
    )
    partial_value = sum_at_owner(whole_grad, "mp", 1)
    emb_grad = sum_at_owner(partial_value, "section", 0).reshape(proj_cols, images)
    pre_grad = (emb_grad * gelu_slope(pre_act).T).astype(jnp.bfloat16)
    return sum_at_owner(
        lax.dot_general(
            features, pre_grad, (((0,), (1,)), ((), ())), preferred_element_type=jnp.float32
        ),
        "dp",
        0,
    )


def solution(mesh):
    placed = (
        P("dp", None),
        P("dp", None),
        P(),
        P("dp", None),
        P("dp"),
        P("dp", None),
        P("dp", None),
        P(None, ("section", "mp")),
        P("section", "mp"),
        P("dp", ("section", "mp")),
        P("dp", ("section", "mp")),
    )
    return jax.shard_map(
        body, mesh=mesh, in_specs=placed, out_specs=P("dp", ("section", "mp")), check_vma=False
    )
```

profile of v0, /device:TPU:1, one launch (start us, length us, event | category | flops | bytes accessed | tf_op | source)
XLA Modules:
  0.0 331.5 jit_solution(18323178748713335903)
XLA Ops:
  0.0 0.0 copy-start
  0.0 0.8 fusion.64
  0.8 1.6 gather_fusion
  2.3 0.1 fusion.51
  2.4 0.2 reduce_window_sum.18
  2.6 0.2 select_reduce_fusion
  2.8 1.1 scatter_custom_fusion
  3.9 0.7 all_to_all.26
  4.7 18.0 %all-to-all-start = ((s32[48,1,5]{2,1,0:T(1,128)}), s32[48,1,5]{2,1,0:T(1,128)S(1)}, u32[]{:S(2)}, u32[]{:S(2)}) async-start(s32[48,1,5]{2,1,0:T(1,128)} %bitcast.4), calls=%async_computation | async-start | bytes 49152 | tf_op jit(solution)/shard_map/all_to_all | solution.py:114
  22.7 0.7 broadcast_bitcast_fusion
  23.4 1.0 constant_dynamic-slice_fusion
  24.4 0.1 dynamic_slice.7
  24.5 8.5 %all-to-all-done = s32[48,1,5]{2,1,0:T(1,128)S(1)} async-done(((s32[48,1,5]{2,1,0:T(1,128)}), s32[48,1,5]{2,1,0:T(1,128)S(1)}, u32[]{:S(2)}, u32[]{:S(2)}) %all-to-all-start) | async-done | bytes 992 | tf_op jit(solution)/shard_map/all_to_all | solution.py:114
  33.0 0.1 reshape.196
  33.2 0.8 gather_fusion.1
  34.0 0.1 reshape.225
  34.2 14.9 %all_to_all.42 = bf16[48,2,180]{2,1,0:T(2,128)(2,1)S(1)} all-to-all(bf16[48,2,180]{2,1,0:T(2,128)(2,1)S(1)} %reshape.225), channel_id=1, replica_groups=mesh['dp'=48,'section'=4,'mp'=4] {'dp'}, dimensions={0} | all-to-all | bytes 69120 | tf_op jit(solution)/shard_map/all_to_all | solution.py:116
  49.0 0.1 reshape.226
  49.2 1.1 gather_fusion.2
  50.3 0.1 copy.64
  50.4 19.3 %all_to_all.43 = bf16[16,128,72]{1,2,0:T(8,128)(2,1)S(1)} all-to-all(bf16[16,128,72]{1,2,0:T(8,128)(2,1)S(1)} %broadcast_in_dim.24), channel_id=1, replica_groups=mesh['dp'=48,'section'=4,'mp'=4] {'section','mp'}, dimensions={0} | all-to-all | bytes 589824 | tf_op jit(solution)/shard_map/all_to_all | solution.py:17
  69.8 0.0 copy-start.2
  69.8 0.7 copy-done.2
  70.5 0.0 copy-done
  70.5 0.0 copy-start.8
  70.5 0.4 fusion.29
  70.9 0.1 copy.65
  71.1 1.8 broadcast_in_dim.25
  72.8 6.1 %all-to-all-start.3 = ((bf16[16,128,512]{1,2,0:T(8,128)(2,1)}), bf16[16,128,512]{1,2,0:T(8,128)(2,1)S(1)}, u32[]{:S(2)}, u32[]{:S(2)}) async-start(bf16[16,128,512]{1,2,0:T(8,128)(2,1)} %broadcast_in_dim.25), calls=%async_computation.3 | async-start | bytes 4194304 | tf_op jit(solution)/shard_map/all_to_all | solution.py:17
  79.0 0.0 copy-done.8
  79.0 0.2 reduce-window.8
  79.2 4.0 %copy.88 = bf16[1024,1024]{0,1:T(8,128)(2,1)} copy(bf16[1024,1024]{1,0:T(8,128)(2,1)} %param.20) | data formatting | bytes 4194304 | tf_op jit(solution)/shard_map/reshape | solution.py:131
  83.1 4.0 %copy.89 = bf16[1024,1024]{0,1:T(8,128)(2,1)} copy(bf16[1024,1024]{1,0:T(8,128)(2,1)} %param.21) | data formatting | bytes 4194304 | tf_op jit(solution)/shard_map/reshape | solution.py:132
  87.1 0.1 convert_reduce_fusion
  87.2 0.0 copy-done.7
  87.2 0.8 broadcast_compare_fusion
  88.0 44.6 %all-to-all-done.3 = bf16[16,128,512]{1,2,0:T(8,128)(2,1)S(1)} async-done(((bf16[16,128,512]{1,2,0:T(8,128)(2,1)}), bf16[16,128,512]{1,2,0:T(8,128)(2,1)S(1)}, u32[]{:S(2)}, u32[]{:S(2)}) %all-to-all-start.3) | async-done | bytes 2097184 | tf_op jit(solution)/shard_map/all_to_all | solution.py:17
  132.6 3.0 fusion.87
  135.6 0.0 copy-start.5
  135.6 0.1 multiply_reduce_fusion.1
  135.8 0.5 copy-done.5
  136.3 6.4 %fusion.82 = (f32[8,1024]{1,0:T(8,128)}, f32[8,1024,128]{1,2,0:T(8,128)}) fusion(pred[1024,128]{0,1:T(8,128)(4,1)} %broadcast_compare_fusion, bf16[1024,8,128]{0,2,1:T(8,128)(2,1)} %bitcast.137, f32[128,256]{1,0:T(8,128)} %copy-done.5, f32[128]{0:T(128)S(1)} %add_rsqrt_fusion), kind=kOutput, calls=%fused_computation.103 | convolution fusion | flops 273711232 | bytes 6652416 | tf_op jit(solution)/shard_map/sub | solution.py:66
  142.7 0.0 copy-done.4
  142.7 3.1 fusion.22
  145.8 0.0 copy-done.6
  145.8 0.5 copy-done.9
  146.3 0.0 copy-done.10
  146.3 1.0 fusion.1
  147.2 0.6 copy-done.3
  147.9 1.1 multiply_reduce_fusion
  149.0 0.1 multiply_convert_fusion.1
  149.1 0.9 copy-done.1
  150.0 3.4 %convolution_bitcast_fusion = f32[8192,128]{0,1:T(8,128)} fusion(bf16[8192,256]{1,0:T(8,128)(2,1)S(1)} %copy-done.1, bf16[128,128]{1,0:T(8,128)(2,1)S(1)} %fusion.22, bf16[128,128]{1,0:T(8,128)(2,1)S(1)} %multiply_convert_fusion.1), kind=kOutput, calls=%fused_computation.5 | convolution fusion | flops 537001984 | bytes 8454144 | tf_op jit(solution)/shard_map/dot_general | solution.py:135
  153.4 6.0 %reshape_reshape.3 = f32[4,4,1,512,128]{3,1,0,4,2:T(4,128)} reshape(f32[8192,128]{0,1:T(8,128)} %convolution_bitcast_fusion) | data formatting | bytes 8388608 | tf_op jit(solution)/shard_map/reshape;reshape | solution.py:28
  159.5 3.8 %copy.91 = f32[4,4,1,512,128]{3,0,4,2,1:T(4,128)S(1)} copy(f32[4,4,1,512,128]{3,1,0,4,2:T(4,128)} %reshape_reshape.3) | data formatting | bytes 8388608 | tf_op jit(solution)/shard_map/reshape;reshape | solution.py:28
  163.3 51.2 %all_to_all.44 = f32[4,4,1,512,128]{3,1,4,2,0:T(4,128)} all-to-all(f32[4,4,1,512,128]{3,1,4,2,0:T(4,128)S(1)} %bitcast.132), channel_id=1, replica_groups=mesh['dp'=48,'section'=4,'mp'=4] {'mp'}, dimensions={0} | all-to-all | bytes 8388608 | tf_op jit(solution)/shard_map/all_to_all | solution.py:34
  214.5 3.2 reduce_sum.90
  217.7 0.4 copy.76
  218.2 24.3 %all_to_all.45 = f32[4,1,1,512,128]{4,3,2,1,0:T(8,128)S(1)} all-to-all(f32[4,1,1,512,128]{4,3,2,1,0:T(8,128)S(1)} %copy.76), channel_id=1, replica_groups=mesh['dp'=48,'section'=4,'mp'=4] {'section'}, dimensions={0} | all-to-all | bytes 2097152 | tf_op jit(solution)/shard_map/all_to_all | solution.py:34
  242.5 0.1 reduce_sum.91
  242.5 0.1 copy.77
  242.7 1.6 fusion.41
  244.2 86.5 %all_to_all.46 = f32[48,24,512]{2,1,0:T(8,128)S(1)} all-to-all(f32[48,24,512]{2,1,0:T(8,128)S(1)} %fusion.41), channel_id=1, replica_groups=mesh['dp'=48,'section'=4,'mp'=4] {'dp'}, dimensions={0} | all-to-all | bytes 4718592 | tf_op jit(solution)/shard_map/all_to_all | solution.py:34
  330.7 0.8 reduce_sum.92
  (17 shorter events, 0.1 us)
Async XLA Ops:
  0.0 70.5 %copy-start = (bf16[1152,512]{1,0:T(8,128)(2,1)S(1)}, bf16[1152,512]{1,0:T(8,128)(2,1)}, u32[]{:S(2)}) copy-start(bf16[1152,512]{1,0:T(8,128)(2,1)} %param.18) | copy-start | bytes 3538948
  4.7 28.3 %all-to-all-start = ((s32[48,1,5]{2,1,0:T(1,128)}), s32[48,1,5]{2,1,0:T(1,128)S(1)}, u32[]{:S(2)}, u32[]{:S(2)}) async-start(s32[48,1,5]{2,1,0:T(1,128)} %bitcast.4), calls=%async_computation | async-start | bytes 49152 | tf_op jit(solution)/shard_map/all_to_all | solution.py:114
  69.8 0.7 copy-start.2
  70.5 8.5 %copy-start.8 = (s32[1,8]{1,0:T(1,128)S(1)}, s32[1,8]{1,0:T(1,128)}, u32[]{:S(2)}) copy-start(s32[1,8]{1,0:T(1,128)} %param.17) | copy-start | bytes 100
  72.8 59.8 %all-to-all-start.3 = ((bf16[16,128,512]{1,2,0:T(8,128)(2,1)}), bf16[16,128,512]{1,2,0:T(8,128)(2,1)S(1)}, u32[]{:S(2)}, u32[]{:S(2)}) async-start(bf16[16,128,512]{1,2,0:T(8,128)(2,1)} %broadcast_in_dim.25), calls=%async_computation.3 | async-start | bytes 4194304 | tf_op jit(solution)/shard_map/all_to_all | solution.py:17
  79.2 8.0 %copy-start.7 = (s32[1,1024]{1,0:T(1,128)S(1)}, s32[1,1024]{1,0:T(1,128)}, u32[]{:S(2)}) copy-start(s32[1,1024]{1,0:T(1,128)} %param.16) | copy-start | bytes 12292
  135.6 0.6 copy-start.5
  136.3 6.4 %copy-start.4 = (bf16[1024,1024]{0,1:T(8,128)(2,1)S(1)}, bf16[1024,1024]{0,1:T(8,128)(2,1)}, u32[]{:S(2)}) copy-start(bf16[1024,1024]{0,1:T(8,128)(2,1)} %copy.89) | copy-start | bytes 6291460
  142.7 3.1 copy-start.6
  142.7 3.5 %copy-start.9 = (f32[8,1024,128]{1,2,0:T(8,128)S(1)}, f32[8,1024,128]{1,2,0:T(8,128)}, u32[]{:S(2)}) copy-start(f32[8,1024,128]{1,2,0:T(8,128)} %get-tuple-element.10) | copy-start | bytes 12582916
  142.7 3.5 %copy-start.10 = (f32[8,1024]{1,0:T(8,128)S(1)}, f32[8,1024]{1,0:T(8,128)}, u32[]{:S(2)}) copy-start(f32[8,1024]{1,0:T(8,128)} %get-tuple-element.9) | copy-start | bytes 98308
  146.3 1.6 copy-start.3
  147.9 2.2 copy-start.1
where the time goes:
time: 332 us; the launch traced here: 331 us
  blocking collectives  196 us (59%)
  waiting for transfers between devices  53.2 us (16%)
  local copies, waits for them, and re-layouts  31.2 us (9%)
  starting transfers between devices  24.1 us (7%)
  matrix products  20 us (6%)
  other arithmetic  6.59 us (2%)
    all_to_all x3, blocking collectives, sum_at_owner(): tiles = lax.all_to_all(split_up(array, dim, peers), axis, 0, 0, tiled=True)  162 us
    all_to_all x1, waiting for transfers between devices, copy_for_each(): lax.all_to_all(jnp.broadcast_to(array[None], (peers, *array.shape)), axis...  44.6 us
    all_to_all x1, blocking collectives, copy_for_each(): lax.all_to_all(jnp.broadcast_to(array[None], (peers, *array.shape)), axis...  19.3 us
    all_to_all x1, starting transfers between devices, body(): lax.all_to_all(wanted, 'dp', split_axis=0, concat_axis=0, tiled=True)  18 us
    all_to_all x1, blocking collectives, body(): lax.all_to_all(scaled, 'dp', split_axis=0, concat_axis=0, tiled=True)  14.9 us
    another operation x2, local copies, waits for them, and re-layouts, split_up(): array.reshape(*dims[:dim], peers, dims[dim] // peers, *dims[dim + 1:])  9.82 us
    all_to_all x1, waiting for transfers between devices, body(): lax.all_to_all(wanted, 'dp', split_axis=0, concat_axis=0, tiled=True)  8.54 us
  transfers between devices with their start and end apart: 2, of which 2 were waited for; matrix products, arithmetic and copies ran while one was open for 3% of the time, Pallas kernels for 0%

commit v1 on v0

--- a/solution.py
+++ b/solution.py
@@ -1,38 +1,16 @@
+import functools
+
 import jax
 import jax.numpy as jnp
 from jax import lax
+from jax.experimental import pallas as pl
+from jax.experimental.pallas import tpu as pltpu
 from jax.sharding import PartitionSpec as P
 
 QBLK = 128
-
-
-def joined_along(tiles, dim):
-    tiles = jnp.moveaxis(tiles, 0, dim)
-    dims = tiles.shape
-    return tiles.reshape(*dims[:dim], dims[dim] * dims[dim + 1], *dims[dim + 2 :])
-
-
-def copy_for_each(array, axis):
-    peers = lax.axis_size(axis)
-    return lax.all_to_all(
-        jnp.broadcast_to(array[None], (peers, *array.shape)), axis, 0, 0, tiled=True
-    )
-
-
-def gathered_copies(array, axis, dim):
-    return joined_along(copy_for_each(array, axis), dim)
-
-
-def split_up(array, dim, peers):
-    dims = array.shape
-    tiles = array.reshape(*dims[:dim], peers, dims[dim] // peers, *dims[dim + 1 :])
-    return jnp.moveaxis(tiles, dim, 0)
-
-
-def sum_at_owner(array, axis, dim):
-    peers = lax.axis_size(axis)
-    tiles = lax.all_to_all(split_up(array, dim, peers), axis, 0, 0, tiled=True)
-    return jnp.sum(tiles, axis=0)
+RING = 4
+STREAMS = ((0, 3, "x"), (3, 6, "x"), (6, 8, "y"))
+AXIS = {"x": "mp", "y": "section"}
 
 
 def gelu(values):
@@ -46,6 +24,375 @@
     return 0.5 * (1.0 + tangent) + 0.5 * values * (1.0 - tangent * tangent) * 0.7978845608028654 * (
         1.0 + 3.0 * 0.044715 * values * values
     )
+
+
+def ring_target(axis, step):
+    name = AXIS[axis]
+    return {name: lax.rem(lax.axis_index(name) + (step + RING) % RING, RING)}
+
+
+def weight_rows(ds, dx, width):
+    s = lax.rem(lax.axis_index("section") + ds, RING)
+    m = lax.rem(lax.axis_index("mp") + dx, RING)
+    return pl.multiple_of((s * RING + m) * width, width)
+
+
+def enter(targets):
+    barrier = pltpu.get_barrier_semaphore()
+    for target in targets:
+        pl.semaphore_signal(barrier, 1, device_id=target, device_id_type=pl.DeviceIdType.MESH)
+    return lambda: pl.semaphore_wait(barrier, len(targets))
+
+
+def remote(src, dst, send_sem, recv_sem, target):
+    return pltpu.make_async_remote_copy(
+        src_ref=src,
+        dst_ref=dst,
+        send_sem=send_sem,
+        recv_sem=recv_sem,
+        device_id=target,
+        device_id_type=pl.DeviceIdType.MESH,
+    )
+
+
+def ring_neighbours():
+    return [ring_target(a, d) for a in "xy" for d in (1, -1)]
+
+
+def forward_kernel(feat_ref, proj_ref, w_ref, pre_ref, kv_ref, gat, send_sem, recv_sem):
+    images, width = pre_ref.shape
+    half = width // 2
+    ready = enter(ring_neighbours())
+    pre = jnp.dot(feat_ref[...], proj_ref[...], preferred_element_type=jnp.float32)
+    pre_ref[...] = pre
+    gat[0, 0] = gelu(pre).astype(jnp.bfloat16)
+    ready()
+
+    def place(first, i, j):
+        return (i, j) if first == "y" else (j, i)
+
+    copies = {}
+    started = []
+
+    def send(c, key, number, axis, step, src, dst):
+        copy = remote(src, dst, send_sem.at[c, number], recv_sem.at[c, number], ring_target(axis, step))
+        copy.start()
+        copies[c, key] = copy
+        started.append(copy)
+
+    def block(c, i, j, part=None):
+        lo, hi, first = streams[c]
+        a, b = place(first, i, j)
+        cols = slice(None) if part is None else slice(part * half, part * half + half)
+        return gat.at[a, b, lo:hi, cols]
+
+    unit = images // 8
+    streams = [(a * unit, b * unit, "y" if f == "x" else "x") for a, b, f in STREAMS]
+    order = (2, 0, 1)
+
+    def second(c, i):
+        lo, hi, first = streams[c]
+        other = "x" if first == "y" else "y"
+        send(c, ("p", i, 0), 4 + 2 * i, other, 1, block(c, i, 0), block(c, i, 3))
+        send(c, ("p", i, 1), 5 + 2 * i, other, -1, block(c, i, 0), block(c, i, 1))
+
+    for c in order:
+        first = streams[c][2]
+        send(c, ("a", 0), 0, first, 1, block(c, 0, 0), block(c, 3, 0))
+        send(c, ("a", 1), 1, first, -1, block(c, 0, 0), block(c, 1, 0))
+    for c in order:
+        second(c, 0)
+    for c in order:
+        first = streams[c][2]
+        copies[c, ("a", 0)].wait_recv()
+        send(c, ("b", 0), 2, first, 1, block(c, 3, 0, 0), block(c, 2, 0, 0))
+        copies[c, ("a", 1)].wait_recv()
+        send(c, ("b", 1), 3, first, -1, block(c, 1, 0, 1), block(c, 2, 0, 1))
+        second(c, 3)
+        second(c, 1)
+    for c in order:
+        copies[c, ("b", 0)].wait_recv()
+        copies[c, ("b", 1)].wait_recv()
+        second(c, 2)
+
+    def forward(c, i, d):
+        lo, hi, first = streams[c]
+        other = "x" if first == "y" else "y"
+        copies[c, ("p", i, d)].wait_recv()
+        source = 3 if d == 0 else 1
+        send(c, ("q", i), 12 + i, other, 1 if d == 0 else -1, block(c, i, source), block(c, i, 2))
+
+    for i, d in ((0, 0), (3, 1), (1, 0), (2, 1)):
+        for c in order:
+            forward(c, i, d)
+
+    def term(ds, dx):
+        rows = pl.ds(weight_rows(ds, dx, width), width)
+        return jnp.dot(gat[ds, dx], w_ref[rows, :], preferred_element_type=jnp.float32)
+
+    kv = term(0, 0)
+    waited = {("p", 0, 0), ("p", 3, 1), ("p", 1, 0), ("p", 2, 1), ("a", 0), ("a", 1), ("b", 0), ("b", 1)}
+    for (c, key), copy in copies.items():
+        if key not in waited:
+            copy.wait_recv()
+    for ds in range(RING):
+        for dx in range(RING):
+            if (ds, dx) != (0, 0):
+                kv = kv + term(ds, dx)
+    kv_ref[...] = kv
+    for copy in started:
+        copy.wait_send()
+
+
+def forward(features, proj_weight, kv_weight):
+    images, width = features.shape[0], proj_weight.shape[1]
+    return pl.pallas_call(
+        forward_kernel,
+        out_shape=(
+            jax.ShapeDtypeStruct((images, width), jnp.float32),
+            jax.ShapeDtypeStruct((images, kv_weight.shape[1]), jnp.float32),
+        ),
+        in_specs=[pl.BlockSpec(memory_space=pltpu.VMEM)] * 3,
+        out_specs=(pl.BlockSpec(memory_space=pltpu.VMEM),) * 2,
+        scratch_shapes=[
+            pltpu.VMEM((RING, RING, images, width), jnp.bfloat16),
+            pltpu.SemaphoreType.DMA((len(STREAMS), 16)),
+            pltpu.SemaphoreType.DMA((len(STREAMS), 16)),
+        ],
+        compiler_params=pltpu.CompilerParams(collective_id=1, has_side_effects=True),
+        name="project_and_gather",
+    )(features, proj_weight, kv_weight)
+
+
+def backward_kernel(kvg_ref, w_ref, pre_ref, ft_ref, out_ref, *scratch):
+    images, width = pre_ref.shape
+    half = width // 2
+    rows, depth = out_ref.shape[0], ft_ref.shape[1]
+    zs = depth // rows
+    part, feat, pgs, sums, zsend, zrecv = scratch[:6]
+    bufs = [scratch[6 + 8 * c : 14 + 8 * c] for c in range(len(STREAMS))]
+    send_sem, recv_sem, dsend_sem, drecv_sem, zsend_sem, zrecv_sem = scratch[6 + 8 * len(STREAMS) :]
+    unit = images // 8
+    streams = [(a * unit, b * unit, f) for a, b, f in STREAMS]
+
+    place = lax.axis_index("dp")
+    core = lax.rem(place, 2)
+    z = lax.rem(place // 2, zs)
+    y = place // (2 * zs)
+
+    def dp_device(yy, zz, cc):
+        return {"dp": (yy * zs + zz) * 2 + cc}
+
+    core_peer = dp_device(y, z, 1 - core)
+    y_peer = dp_device(1 - y, z, core)
+    both_peer = dp_device(1 - y, z, 1 - core)
+    z_at = [lax.rem(z + dz, zs) for dz in range(zs)]
+    z_peers = [dp_device(y, z_at[dz], core) for dz in range(1, zs)]
+    ready = enter(ring_neighbours() + [core_peer, y_peer, both_peer] + z_peers)
+
+    def partial(ds, dx):
+        block = w_ref[pl.ds(weight_rows(ds, dx, width), width), :]
+        part[ds, dx] = lax.dot_general(
+            kvg_ref[...], block, (((1,), (1,)), ((), ())), preferred_element_type=jnp.float32
+        )
+
+    early = [(2, 2)] + [(ds, 2) for ds in (0, 1, 3)] + [(2, dx) for dx in (0, 1, 3)]
+    for ds, dx in early:
+        partial(ds, dx)
+    copies = {}
+    started = []
+
+    def ring_send(c, k, d, axis, src, dst):
+        n = 2 * k + d
+        copy = remote(src, dst, send_sem.at[c, n], recv_sem.at[c, n], ring_target(axis, 1 if d == 0 else -1))
+        copy.start()
+        copies[c, k, d] = copy
+        started.append(copy)
+
+    def own(c, i, j):
+        lo, hi, first = streams[c]
+        a, b = (j, i) if first == "x" else (i, j)
+        return part.at[a, b, lo:hi, :]
+
+    def step1(c):
+        a1s, a1r = bufs[c][:2]
+        for d in (0, 1):
+            for n in (0, 1):
+                a1s[d, n] = own(c, 2, 2 * d + n)[...].astype(jnp.bfloat16)
+            ring_send(c, 0, d, streams[c][2], a1s.at[d], a1r.at[d])
+
+    def step2(c):
+        a1r, a2s, a2r = bufs[c][1:4]
+        for d in (0, 1):
+            copies[c, 0, d].wait_recv()
+            for j in range(RING):
+                value = own(c, 1 if d == 0 else 3, j)[...]
+                if j // 2 == d:
+                    value = value + a1r[d, j % 2].astype(jnp.float32)
+                a2s[d, j] = value.astype(jnp.bfloat16)
+            ring_send(c, 1, d, streams[c][2], a2s.at[d], a2r.at[d])
+
+    def step3(c):
+        a2r, b1s, b1r = bufs[c][3:6]
+        other = "y" if streams[c][2] == "x" else "x"
+        for d in (0, 1):
+            copies[c, 1, d].wait_recv()
+        for j in (2, 1, 3, 0):
+            ref = own(c, 0, j)
+            ref[...] = ref[...] + a2r[0, j].astype(jnp.float32) + a2r[1, j].astype(jnp.float32)
+            if j == 2:
+                for d in (0, 1):
+                    b1s[d] = ref[:, d * half : (d + 1) * half].astype(jnp.bfloat16)
+                    ring_send(c, 2, d, other, b1s.at[d], b1r.at[d])
+
+    def step4(c):
+        b1r, b2s, b2r = bufs[c][5:8]
+        other = "y" if streams[c][2] == "x" else "x"
+        for d in (0, 1):
+            copies[c, 2, d].wait_recv()
+            ref = own(c, 0, 1 if d == 0 else 3)
+            for n in (0, 1):
+                value = ref[:, n * half : (n + 1) * half]
+                if n == d:
+                    value = value + b1r[d].astype(jnp.float32)
+                b2s[d, :, n * half : (n + 1) * half] = value.astype(jnp.bfloat16)
+            ring_send(c, 3, d, other, b2s.at[d], b2r.at[d])
+
+    def dp_send(c, k, src, dst, target):
+        copy = remote(src, dst, dsend_sem.at[c, k], drecv_sem.at[c, k], target)
+        copy.start()
+        copies["dp", c, k] = copy
+        started.append(copy)
+
+    def pg_rows(c, k):
+        lo, hi, _ = streams[c]
+        return pgs.at[k * images + lo : k * images + hi, :]
+
+    def finish(c):
+        lo, hi, _ = streams[c]
+        b2r = bufs[c][7]
+        for d in (0, 1):
+            copies[c, 3, d].wait_recv()
+        total = own(c, 0, 0)[...] + b2r[0].astype(jnp.float32) + b2r[1].astype(jnp.float32)
+        pg_rows(c, 0)[...] = (total * gelu_slope(pre_ref[lo:hi, :])).astype(jnp.bfloat16)
+        dp_send(c, 0, pg_rows(c, 0), pg_rows(c, 2), y_peer)
+        dp_send(c, 1, pg_rows(c, 0), pg_rows(c, 1), core_peer)
+
+    def relay(c):
+        copies["dp", c, 0].wait_recv()
+        dp_send(c, 2, pg_rows(c, 2), pg_rows(c, 3), core_peer)
+
+    ready()
+    for c in (2, 0, 1):
+        step1(c)
+    last = len(STREAMS)
+    for k, (yy, cc, target) in enumerate(
+        ((y, 1 - core, core_peer), (1 - y, core, y_peer), (1 - y, 1 - core, both_peer))
+    ):
+        dp_send(
+            last, k, ft_ref.at[yy * 2 + cc], feat.at[:, (k + 1) * images : (k + 2) * images], target
+        )
+    for ds in range(RING):
+        for dx in range(RING):
+            if (ds, dx) not in early:
+                partial(ds, dx)
+    feat[:, 0:images] = ft_ref[y * 2 + core]
+    step2(0), step2(2), step2(1)
+    step3(0), step3(2), step4(0), step4(2), step3(1), finish(2), finish(0), step4(1)
+    relay(2), relay(0), finish(1), relay(1)
+    for c in range(last):
+        copies["dp", c, 1].wait_recv()
+        copies["dp", c, 2].wait_recv()
+    for k in range(3):
+        copies["dp", last, k].wait_recv()
+    sums[...] = jnp.dot(feat[...], pgs[...], preferred_element_type=jnp.float32)
+
+    def folded(dz):
+        value = sums[pl.ds(pl.multiple_of(z_at[dz] * rows, rows), rows), :]
+        return jnp.concatenate([value[:, :half], value[:, half:]], axis=0)
+
+    zcopies = []
+    far_first = sorted(range(1, zs), key=lambda dz: -min(dz, zs - dz))
+    for dz in far_first:
+        zsend[dz] = folded(dz).astype(jnp.bfloat16)
+        copy = remote(zsend.at[dz], zrecv.at[dz], zsend_sem.at[dz], zrecv_sem.at[dz], z_peers[dz - 1])
+        copy.start()
+        zcopies.append(copy)
+        started.append(copy)
+    total = folded(0)
+    for dz, copy in sorted(zip(far_first, zcopies), key=lambda item: min(item[0], zs - item[0])):
+        copy.wait_recv()
+        total = total + zrecv[dz].astype(jnp.float32)
+    out_ref[:, :half] = total[:rows]
+    out_ref[:, half:] = total[rows:]
+    for copy in started:
+        copy.wait_send()
+
+
+def backward(kv_grad, kv_weight, pre_act, feature_rows):
+    images, width = pre_act.shape
+    depth = feature_rows.shape[1]
+    groups = lax.axis_size("dp")
+    rows = 4 * depth // groups
+    zs = depth // rows
+    half = width // 2
+    unit = images // 8
+    bf16 = jnp.bfloat16
+    ring_bufs = []
+    for a, b, _ in STREAMS:
+        n = (b - a) * unit
+        ring_bufs += [pltpu.VMEM((2, 2, n, width), bf16)] * 2
+        ring_bufs += [pltpu.VMEM((2, RING, n, width), bf16)] * 2
+        ring_bufs += [pltpu.VMEM((2, n, half), bf16)] * 2
+        ring_bufs += [pltpu.VMEM((2, n, width), bf16)] * 2
+    return pl.pallas_call(
+        backward_kernel,
+        out_shape=jax.ShapeDtypeStruct((rows, width), jnp.float32),
+        in_specs=[pl.BlockSpec(memory_space=pltpu.VMEM)] * 4,
+        out_specs=pl.BlockSpec(memory_space=pltpu.VMEM),
+        scratch_shapes=[
+            pltpu.VMEM((RING, RING, images, width), jnp.float32),
+            pltpu.VMEM((depth, 4 * images), bf16),
+            pltpu.VMEM((4 * images, width), bf16),
+            pltpu.VMEM((depth, width), jnp.float32),
+            pltpu.VMEM((zs, 2 * rows, half), bf16),
+            pltpu.VMEM((zs, 2 * rows, half), bf16),
+            *ring_bufs,
+            pltpu.SemaphoreType.DMA((len(STREAMS), 8)),
+            pltpu.SemaphoreType.DMA((len(STREAMS), 8)),
+            pltpu.SemaphoreType.DMA((len(STREAMS) + 1, 3)),
+            pltpu.SemaphoreType.DMA((len(STREAMS) + 1, 3)),
+            pltpu.SemaphoreType.DMA((zs,)),
+            pltpu.SemaphoreType.DMA((zs,)),
+        ],
+        compiler_params=pltpu.CompilerParams(collective_id=2, has_side_effects=True),
+        name="reduce_gradients",
+    )(kv_grad, kv_weight, pre_act, feature_rows)
+
+
+def feature_rows_of(features):
+    images, vis = features.shape
+    groups = lax.axis_size("dp")
+    zs, rows = groups // 4, vis // groups
+    tiles = features.T.reshape(2, zs, 2, rows, images)
+    return jnp.moveaxis(tiles, 2, 1).reshape(4, zs * rows, images)
+
+
+def joined_along(tiles, dim):
+    tiles = jnp.moveaxis(tiles, 0, dim)
+    dims = tiles.shape
+    return tiles.reshape(*dims[:dim], dims[dim] * dims[dim + 1], *dims[dim + 2 :])
+
+
+def copy_for_each(array, axis):
+    peers = lax.axis_size(axis)
+    return lax.all_to_all(
+        jnp.broadcast_to(array[None], (peers, *array.shape)), axis, 0, 0, tiled=True
+    )
+
+
+def gathered_copies(array, axis, dim):
+    return joined_along(copy_for_each(array, axis), dim)
 
 
 def head_backward(query_heads, grad_heads, key_value, token_doc, image_doc):
@@ -116,13 +463,7 @@
     arrived = lax.all_to_all(scaled, "dp", split_axis=0, concat_axis=0, tiled=True)
     features = arrived[owner_dev, slot_index]
     features = gathered_copies(features, ("section", "mp"), 1)
-    pre_act = jnp.dot(features, proj_weight, preferred_element_type=jnp.float32)
-    embedded = gelu(pre_act).astype(jnp.bfloat16)
-    key_value = jnp.dot(
-        gathered_copies(embedded, ("section", "mp"), 1),
-        kv_weight,
-        preferred_element_type=jnp.float32,
-    )
+    pre_act, key_value = forward(features, proj_weight, kv_weight)
     doc_ends = jnp.cumsum(image_count[0])
     positions = jnp.arange(images, dtype=jnp.int32)
     image_doc = jnp.sum((doc_ends[None, :] <= positions[:, None]).astype(jnp.int32), axis=1)
@@ -131,23 +472,7 @@
     query_heads = queries.reshape(tokens, -1, head_size)
     grad_heads = out_grad.reshape(tokens, -1, head_size)
     kv_grad = head_backward(query_heads, grad_heads, key_value, text_doc[0], image_doc)
-    proj_cols = proj_weight.shape[1]
-    whole_grad = lax.dot_general(
-        kv_weight, kv_grad, (((1,), (1,)), ((), ())), preferred_element_type=jnp.float32
-    )
-    whole_grad = whole_grad.reshape(
-        lax.axis_size("section"), lax.axis_size("mp"), proj_cols, images
-    )
-    partial_value = sum_at_owner(whole_grad, "mp", 1)
-    emb_grad = sum_at_owner(partial_value, "section", 0).reshape(proj_cols, images)
-    pre_grad = (emb_grad * gelu_slope(pre_act).T).astype(jnp.bfloat16)
-    return sum_at_owner(
-        lax.dot_general(
-            features, pre_grad, (((0,), (1,)), ((), ())), preferred_element_type=jnp.float32
-        ),
-        "dp",
-        0,
-    )
+    return backward(kv_grad, kv_weight, pre_act, feature_rows_of(features))
 
 
 def solution(mesh):

time: 332 us -> 167 us (0.50)
  blocking collectives: 196 us -> 14.9 us
  Pallas kernels: 0 us -> 79.4 us
  waiting for transfers between devices: 53.2 us -> 13.5 us
  local copies, waits for them, and re-layouts: 31.2 us -> 18.1 us
  matrix products: 20 us -> 10.8 us
    all_to_all x4 -> x0, blocking collectives: 181 us -> none  [the longest x3 162 us: sum_at_owner(): tiles = lax.all_to_all(split_up(array, dim, peers), axis, 0, 0, tiled=True)]
    pallas_call x0 -> x2, Pallas kernels: none -> 79.4 us  [the longest x1 51.4 us: backward(): pl.pallas_call(backward_kernel, out_shape=jax.ShapeDtypeStruct((rows, wid...]
    all_to_all x1, waiting for transfers between devices: 44.6 us -> 4.1 us  [copy_for_each(): lax.all_to_all(jnp.broadcast_to(array[None], (peers, *array.shape)), axis...]
    another operation x2 -> x0, local copies, waits for them, and re-layouts: 9.82 us -> none  [split_up(): array.reshape(*dims[:dim], peers, dims[dim] // peers, *dims[dim + 1:])]
    dot_general x4 -> x0, matrix products: 8.44 us -> none  [the longest x1 3.41 us: body(): lax.dot_general(kv_weight, kv_grad, (((1,), (1,)), ((), ())), preferred_e...]
    reduce_sum x3 -> x0, other arithmetic: 4.07 us -> none  [sum_at_owner(): return jnp.sum(tiles, axis=0)]
  transfers between devices with their start and end apart: 2 -> 2, of which waited for: 2 -> 2; matrix products, arithmetic and copies ran while one was open for 3% -> 5% of each run, Pallas kernels for 0% -> 0%
where the time goes in v1:
time: 167 us
  Pallas kernels  79.4 us (48%)
  starting transfers between devices  26.5 us (16%)
  local copies, waits for them, and re-layouts  18.1 us (11%)
  blocking collectives  14.9 us (9%)
  waiting for transfers between devices  13.5 us (8%)
  matrix products  10.8 us (6%)
  other arithmetic  3.4 us (2%)
    pallas_call x1, Pallas kernels, backward(): pl.pallas_call(backward_kernel, out_shape=jax.ShapeDtypeStruct((rows, wid...  51.4 us
    pallas_call x1, Pallas kernels, forward(): pl.pallas_call(forward_kernel, out_shape=(jax.ShapeDtypeStruct((images, w...  28 us
    all_to_all x1, starting transfers between devices, body(): lax.all_to_all(wanted, 'dp', split_axis=0, concat_axis=0, tiled=True)  18 us
    all_to_all x1, blocking collectives, body(): lax.all_to_all(scaled, 'dp', split_axis=0, concat_axis=0, tiled=True)  14.9 us
    all_to_all x1, waiting for transfers between devices, body(): lax.all_to_all(wanted, 'dp', split_axis=0, concat_axis=0, tiled=True)  9.43 us
    all_to_all x1, starting transfers between devices, copy_for_each(): lax.all_to_all(jnp.broadcast_to(array[None], (peers, *array.shape)), axis...  8.49 us
    sub x1, matrix products, head_backward(): raised = jnp.where(same_doc, jnp.exp(scores - row_max), 0.0)  4.92 us
    all_to_all x1, waiting for transfers between devices, copy_for_each(): lax.all_to_all(jnp.broadcast_to(array[None], (peers, *array.shape)), axis...  4.1 us
  transfers between devices with their start and end apart: 2, of which 2 were waited for; matrix products, arithmetic and copies ran while one was open for 5% of the time, Pallas kernels for 0%

profile of v1, /device:TPU:1, one launch (start us, length us, event | category | flops | bytes accessed | tf_op | source)
XLA Modules:
  0.0 166.8 jit_solution(4902237142270141738)
XLA Ops:
  0.0 0.0 copy-start
  0.0 0.0 copy-start.6
  0.0 0.0 copy-start.1
  0.0 0.8 fusion.40
  0.8 1.6 gather_fusion
  2.4 0.1 fusion.27
  2.5 0.2 reduce_window_sum.18
  2.7 0.2 select_reduce_fusion
  2.9 1.1 scatter_custom_fusion
  4.0 0.7 all_to_all.14
  4.7 18.0 %all-to-all-start = ((s32[48,1,5]{2,1,0:T(1,128)}), s32[48,1,5]{2,1,0:T(1,128)S(1)}, u32[]{:S(2)}, u32[]{:S(2)}) async-start(s32[48,1,5]{2,1,0:T(1,128)} %bitcast.4), calls=%async_computation | async-start | bytes 49152 | tf_op jit(solution)/shard_map/all_to_all | solution.py:461
  22.7 0.7 broadcast_bitcast_fusion
  23.5 0.0 copy-done
  23.5 0.1 constant_dynamic-slice_fusion
  23.6 0.1 dynamic_slice.7
  23.7 9.4 %all-to-all-done = s32[48,1,5]{2,1,0:T(1,128)S(1)} async-done(((s32[48,1,5]{2,1,0:T(1,128)}), s32[48,1,5]{2,1,0:T(1,128)S(1)}, u32[]{:S(2)}, u32[]{:S(2)}) %all-to-all-start) | async-done | bytes 992 | tf_op jit(solution)/shard_map/all_to_all | solution.py:461
  33.1 0.1 reshape.188
  33.2 0.8 gather_fusion.1
  34.1 0.1 reshape.216
  34.2 14.9 %all_to_all.22 = bf16[48,2,180]{2,1,0:T(2,128)(2,1)S(1)} all-to-all(bf16[48,2,180]{2,1,0:T(2,128)(2,1)S(1)} %reshape.216), channel_id=1, replica_groups=mesh['dp'=48,'section'=4,'mp'=4] {'dp'}, dimensions={0} | all-to-all | bytes 69120 | tf_op jit(solution)/shard_map/all_to_all | solution.py:463
  49.1 0.1 reshape.217
  49.3 1.1 gather_fusion.2
  50.3 0.1 copy.49
  50.4 0.8 broadcast_in_dim.22
  51.2 8.5 %all-to-all-start.2 = ((bf16[16,128,72]{1,2,0:T(8,128)(2,1)}), bf16[16,128,72]{1,2,0:T(8,128)(2,1)S(1)}, u32[]{:S(2)}, u32[]{:S(2)}) async-start(bf16[16,128,72]{1,2,0:T(8,128)(2,1)} %broadcast_in_dim.22), calls=%async_computation.2 | async-start | bytes 589824 | tf_op jit(solution)/shard_map/all_to_all | solution.py:389
  59.7 0.0 copy-done.6
  59.7 0.2 reduce-window.8
  59.9 0.0 copy-done.1
  59.9 0.0 copy-start.5
  59.9 2.6 %copy.66 = bf16[1024,1024]{0,1:T(8,128)(2,1)} copy(bf16[1024,1024]{1,0:T(8,128)(2,1)S(1)} %copy-done.1) | data formatting | bytes 4194304 | tf_op jit(solution)/shard_map/reshape | solution.py:472
  62.5 3.9 %copy.67 = bf16[1024,1024]{0,1:T(8,128)(2,1)} copy(bf16[1024,1024]{1,0:T(8,128)(2,1)} %param.21) | data formatting | bytes 4194304 | tf_op jit(solution)/shard_map/reshape | solution.py:473
  66.4 0.0 copy-start.2
  66.4 0.1 convert_reduce_fusion
  66.5 0.0 copy-done.5
  66.5 0.1 broadcast_compare_fusion
  66.7 4.1 %all-to-all-done.2 = bf16[16,128,72]{1,2,0:T(8,128)(2,1)S(1)} async-done(((bf16[16,128,72]{1,2,0:T(8,128)(2,1)}), bf16[16,128,72]{1,2,0:T(8,128)(2,1)S(1)}, u32[]{:S(2)}, u32[]{:S(2)}) %all-to-all-start.2) | async-done | bytes 294944 | tf_op jit(solution)/shard_map/all_to_all | solution.py:389
  70.8 0.9 copy.50.feat_ref
  71.7 28.0 %project_and_gather.1 = (f32[128,512]{1,0:T(8,128)}, f32[128,256]{1,0:T(8,128)}) custom-call(bf16[128,1152]{1,0:T(8,128)(2,1)} %copy.50.feat_ref, bf16[1152,512]{1,0:T(8,128)(2,1)} %proj_ref.1, bf16[8192,256]{1,0:T(8,128)(2,1)} %w_ref.3), custom_call_target="tpu_custom_call" | custom-call | tf_op jit(solution)/shard_map/project_and_gather/pallas_call | solution.py:149
  99.7 0.9 multiply_reduce_fusion.1
  100.7 0.0 copy-done.2
  100.7 4.9 %fusion.52 = (f32[8,1024]{1,0:T(8,128)S(1)}, f32[8,1024,128]{1,2,0:T(8,128)}) fusion(pred[1024,128]{0,1:T(8,128)(4,1)S(1)} %broadcast_compare_fusion, bf16[1024,8,128]{0,2,1:T(8,128)(2,1)S(1)} %bitcast.102, f32[128,256]{1,0:T(8,128)} %get-tuple-element.7, f32[128]{0:T(128)S(1)} %add_rsqrt_fusion), kind=kOutput, calls=%fused_computation.69 | convolution fusion | flops 273711232 | bytes 6652416 | tf_op jit(solution)/shard_map/sub | solution.py:413
  105.6 0.0 copy-start.3
  105.6 0.0 copy-start.4
  105.6 0.0 copy-start.7
  105.6 3.7 %fusion.22 = bf16[128,128]{1,0:T(8,128)(2,1)S(1)} fusion(bf16[1024,8,128]{0,2,1:T(8,128)(2,1)} %bitcast.104, f32[8,1024,128]{1,2,0:T(8,128)} %get-tuple-element.12, f32[8,1024]{1,0:T(8,128)S(1)} %get-tuple-element.11), kind=kOutput, calls=%fused_computation.24 | convolution fusion | flops 270548992 | bytes 6356992 | tf_op jit(solution)/shard_map/gti,tgd->id/dot_general | solution.py:419
  109.3 0.0 copy-done.3
  109.3 0.0 copy-done.4
  109.3 1.0 copy-done.7
  110.3 1.0 fusion.1
  111.3 0.7 copy.59
  112.0 1.2 multiply_reduce_fusion
  113.2 0.1 multiply_convert_fusion.1
  113.3 0.6 pad_maximum_fusion.kvg_ref
  114.0 51.4 %reduce_gradients.1 = f32[24,512]{1,0:T(8,128)} custom-call(bf16[128,256]{1,0:T(8,128)(2,1)} %pad_maximum_fusion.kvg_ref, bf16[8192,256]{1,0:T(8,128)(2,1)} %w_ref.3, f32[128,512]{1,0:T(8,128)} %get-tuple-element.8.pre_ref, bf16[4,288,128]{2,1,0:T(8,128)(2,1)} %bitcast.106), custom_call_target="tpu_custom_call" | custom-call | tf_op jit(solution)/shard_map/reduce_gradients/pallas_call | solution.py:348
  165.4 1.4 copy.69
  (9 shorter events, 0.1 us)
Async XLA Ops:
  0.0 23.5 %copy-start = (bf16[256,1152]{1,0:T(8,128)(2,1)S(1)}, bf16[256,1152]{1,0:T(8,128)(2,1)}, u32[]{:S(2)}) copy-start(bf16[256,1152]{1,0:T(8,128)(2,1)} %param.11) | copy-start | bytes 1769476
  0.0 59.7 %copy-start.6 = (s32[1,8]{1,0:T(1,128)S(1)}, s32[1,8]{1,0:T(1,128)}, u32[]{:S(2)}) copy-start(s32[1,8]{1,0:T(1,128)} %param.17) | copy-start | bytes 100
  0.0 59.9 %copy-start.1 = (bf16[1024,1024]{1,0:T(8,128)(2,1)S(1)}, bf16[1024,1024]{1,0:T(8,128)(2,1)}, u32[]{:S(2)}) copy-start(bf16[1024,1024]{1,0:T(8,128)(2,1)} %param.20) | copy-start | bytes 6291460
  4.7 28.3 %all-to-all-start = ((s32[48,1,5]{2,1,0:T(1,128)}), s32[48,1,5]{2,1,0:T(1,128)S(1)}, u32[]{:S(2)}, u32[]{:S(2)}) async-start(s32[48,1,5]{2,1,0:T(1,128)} %bitcast.4), calls=%async_computation | async-start | bytes 49152 | tf_op jit(solution)/shard_map/all_to_all | solution.py:461
  51.2 19.5 %all-to-all-start.2 = ((bf16[16,128,72]{1,2,0:T(8,128)(2,1)}), bf16[16,128,72]{1,2,0:T(8,128)(2,1)S(1)}, u32[]{:S(2)}, u32[]{:S(2)}) async-start(bf16[16,128,72]{1,2,0:T(8,128)(2,1)} %broadcast_in_dim.22), calls=%async_computation.2 | async-start | bytes 589824 | tf_op jit(solution)/shard_map/all_to_all | solution.py:389
  59.9 6.6 %copy-start.5 = (s32[1,1024]{1,0:T(1,128)S(1)}, s32[1,1024]{1,0:T(1,128)}, u32[]{:S(2)}) copy-start(s32[1,1024]{1,0:T(1,128)} %param.16) | copy-start | bytes 12292
  66.4 34.2 %copy-start.2 = (bf16[1024,1024]{0,1:T(8,128)(2,1)S(1)}, bf16[1024,1024]{0,1:T(8,128)(2,1)}, u32[]{:S(2)}) copy-start(bf16[1024,1024]{0,1:T(8,128)(2,1)} %copy.66) | copy-start | bytes 6291460
  105.6 3.7 %copy-start.3 = (bf16[1024,1024]{0,1:T(8,128)(2,1)S(1)}, bf16[1024,1024]{0,1:T(8,128)(2,1)}, u32[]{:S(2)}) copy-start(bf16[1024,1024]{0,1:T(8,128)(2,1)} %copy.67) | copy-start | bytes 6291460
  105.6 3.7 %copy-start.4 = (f32[128,256]{1,0:T(8,128)S(1)}, f32[128,256]{1,0:T(8,128)}, u32[]{:S(2)}) copy-start(f32[128,256]{1,0:T(8,128)} %get-tuple-element.7) | copy-start | bytes 393220
  105.6 4.7 %copy-start.7 = (f32[8,1024,128]{1,2,0:T(8,128)S(1)}, f32[8,1024,128]{1,2,0:T(8,128)}, u32[]{:S(2)}) copy-start(f32[8,1024,128]{1,2,0:T(8,128)} %get-tuple-element.12) | copy-start | bytes 12582916

commit v2 on v1

--- a/solution.py
+++ b/solution.py
@@ -59,14 +59,137 @@
     return [ring_target(a, d) for a in "xy" for d in (1, -1)]
 
 
-def forward_kernel(feat_ref, proj_ref, w_ref, pre_ref, kv_ref, gat, send_sem, recv_sem):
+def forward_kernel(
+    owner_ref, shard_ref, row_ref, bank_ref, scale_ref, proj_ref, w_ref,
+    pre_ref, kv_ref, feat_ref,
+    gat, wsend, wrecv, spread, rsend, rrecv, fgat,
+    send_sem, recv_sem, wsend_sem, wrecv_sem, rsend_sem, rrecv_sem, fsend_sem, frecv_sem,
+):
     images, width = pre_ref.shape
     half = width // 2
-    ready = enter(ring_neighbours())
-    pre = jnp.dot(feat_ref[...], proj_ref[...], preferred_element_type=jnp.float32)
+    groups, slots = rsend.shape[:2]
+    bank = bank_ref.shape[0]
+    blocks = fgat.shape[0]
+    here = lax.axis_index("dp")
+    member = lax.axis_index("section") * RING + lax.axis_index("mp")
+    block_at = lax.rem(member, blocks)
+    f32, bf16 = jnp.float32, jnp.bfloat16
+
+    def dp_peer(step):
+        return {"dp": lax.rem(here + step, groups)}
+
+    others = [(ds, dx) for ds in range(RING) for dx in range(RING) if ds or dx]
+
+    def other(ds, dx):
+        return {**ring_target("y", ds), **ring_target("x", dx)}
+
+    barrier = pltpu.get_barrier_semaphore()
+
+    def greet(step, _):
+        pl.semaphore_signal(barrier, 1, device_id=dp_peer(step), device_id_type=pl.DeviceIdType.MESH)
+        return 0
+
+    lax.fori_loop(1, groups, greet, 0)
+    for ds, dx in others:
+        pl.semaphore_signal(barrier, 1, device_id=other(ds, dx), device_id_type=pl.DeviceIdType.MESH)
+
+    def iota(shape, dim):
+        return lax.broadcasted_iota(jnp.int32, shape, dim)
+
+    names_shard = (iota((groups, images), 0) == shard_ref[...]).astype(bf16)
+    owner = jnp.dot(
+        jnp.broadcast_to(owner_ref[...].astype(f32), (8, groups)).astype(bf16),
+        names_shard,
+        preferred_element_type=f32,
+    )[0:1].astype(jnp.int32)
+    ahead = owner - here
+    ahead = jnp.where(ahead < 0, ahead + groups, ahead)
+    chosen = iota((groups, images), 0) == ahead
+    chosen_low = chosen.astype(bf16)
+    before = (iota((images, images), 0) < iota((images, images), 1)).astype(bf16)
+    earlier = jnp.dot(chosen_low, before, preferred_element_type=f32)
+    slot = jnp.sum(jnp.where(chosen, earlier, 0.0), axis=0, keepdims=True).astype(jnp.int32)
+    row_in_slot = jnp.where(iota((QBLK, images), 0) == slot, row_ref[...], 0).astype(f32).astype(bf16)
+    wanted = lax.dot_general(
+        chosen_low, row_in_slot, (((1,), (1,)), ((), ())), preferred_element_type=f32
+    )
+    for step in range(groups):
+        wsend[step] = wanted[step : step + 1, :]
+
+    pl.semaphore_wait(barrier, groups - 1 + len(others))
+
+    def request(step):
+        return remote(
+            wsend.at[step], wrecv.at[step], wsend_sem.at[step], wrecv_sem.at[step], dp_peer(step)
+        )
+
+    def answer(step):
+        return remote(
+            rsend.at[step], rrecv.at[step], rsend_sem.at[step], rrecv_sem.at[step], dp_peer(groups - step)
+        )
+
+    def every_step(do):
+        def run(step, _):
+            do(step)
+            return 0
+
+        lax.fori_loop(1, groups, run, 0)
+
+    every_step(lambda step: request(step).start())
+
+    def expand(step, row):
+        spread[pl.ds(pl.multiple_of(step * slots, slots), slots), :] = jnp.broadcast_to(row, (slots, QBLK))
+
+    expand(0, wsend[0])
+
+    def received(step):
+        request(step).wait_recv()
+        expand(step, wrecv[step])
+
+    every_step(received)
+
+    entries = groups * slots
+    own_slot = lax.rem(iota((entries, QBLK), 0), slots) == iota((entries, QBLK), 1)
+    row = jnp.sum(jnp.where(own_slot, spread[...], 0.0), axis=1, keepdims=True)
+    picks = (row == iota((entries, bank), 1).astype(f32)).astype(bf16)
+    columns = pl.ds(pl.multiple_of(block_at * QBLK, QBLK), QBLK)
+    looked = jnp.dot(picks, bank_ref[:, columns], preferred_element_type=f32)
+    scaled = looked * scale_ref[0, block_at]
+    rsend[...] = scaled.reshape(groups, slots, QBLK).astype(bf16)
+
+    def block_copy(ds, dx):
+        n = ds * RING + dx
+        return remote(
+            fgat.at[block_at], fgat.at[block_at], fsend_sem.at[n], frecv_sem.at[block_at], other(ds, dx)
+        )
+
+    @pl.when(member < blocks)
+    def _():
+        every_step(lambda step: answer(step).start())
+        rrecv[0] = rsend[0]
+        at = iota((entries, images), 0)
+        selected = (at == ahead * slots + slot).astype(bf16)
+        every_step(lambda step: answer(step).wait_recv())
+        arrived = rrecv[...].astype(f32).reshape(entries, QBLK).astype(bf16)
+        fgat[block_at] = lax.dot_general(
+            selected, arrived, (((0,), (0,)), ((), ())), preferred_element_type=f32
+        ).astype(bf16)
+        for ds, dx in others:
+            block_copy(ds, dx).start()
+
+    pre = jnp.zeros((images, width), f32)
+    for b in range(blocks):
+        @pl.when(member != b)
+        def _():
+            remote(
+                fgat.at[b], fgat.at[b], fsend_sem.at[0], frecv_sem.at[b], other(0, 1)
+            ).wait_recv()
+
+        values = fgat[b]
+        feat_ref[:, b * QBLK : (b + 1) * QBLK] = values
+        pre = pre + jnp.dot(values, proj_ref[b * QBLK : (b + 1) * QBLK, :], preferred_element_type=f32)
     pre_ref[...] = pre
-    gat[0, 0] = gelu(pre).astype(jnp.bfloat16)
-    ready()
+    gat[0, 0] = gelu(pre).astype(bf16)
 
     def place(first, i, j):
         return (i, j) if first == "y" else (j, i)
@@ -142,29 +265,109 @@
     kv_ref[...] = kv
     for copy in started:
         copy.wait_send()
-
-
-def forward(features, proj_weight, kv_weight):
-    images, width = features.shape[0], proj_weight.shape[1]
+    every_step(lambda step: request(step).wait_send())
+
+    @pl.when(member < blocks)
+    def _():
+        every_step(lambda step: answer(step).wait_send())
+        for ds, dx in others:
+            block_copy(ds, dx).wait_send()
+
+
+def forward(shard_owner, image_shard, image_row, feature_bank, feature_scale, proj_weight, kv_weight):
+    images, width = image_row.shape[0], proj_weight.shape[1]
+    groups, vis = shard_owner.shape[0], proj_weight.shape[0]
+    slots = 8
+    f32, bf16 = jnp.float32, jnp.bfloat16
+    vmem = pl.BlockSpec(memory_space=pltpu.VMEM)
     return pl.pallas_call(
         forward_kernel,
         out_shape=(
-            jax.ShapeDtypeStruct((images, width), jnp.float32),
-            jax.ShapeDtypeStruct((images, kv_weight.shape[1]), jnp.float32),
+            jax.ShapeDtypeStruct((images, width), f32),
+            jax.ShapeDtypeStruct((images, kv_weight.shape[1]), f32),
+            jax.ShapeDtypeStruct((images, vis), bf16),
         ),
-        in_specs=[pl.BlockSpec(memory_space=pltpu.VMEM)] * 3,
-        out_specs=(pl.BlockSpec(memory_space=pltpu.VMEM),) * 2,
+        in_specs=[vmem] * 4 + [pl.BlockSpec(memory_space=pltpu.SMEM)] + [vmem] * 2,
+        out_specs=(vmem,) * 3,
         scratch_shapes=[
-            pltpu.VMEM((RING, RING, images, width), jnp.bfloat16),
+            pltpu.VMEM((RING, RING, images, width), bf16),
+            pltpu.VMEM((groups, 1, QBLK), f32),
+            pltpu.VMEM((groups, 1, QBLK), f32),
+            pltpu.VMEM((groups * slots, QBLK), f32),
+            pltpu.VMEM((groups, slots, QBLK), bf16),
+            pltpu.VMEM((groups, slots, QBLK), bf16),
+            pltpu.VMEM((vis // QBLK, images, QBLK), bf16),
             pltpu.SemaphoreType.DMA((len(STREAMS), 16)),
             pltpu.SemaphoreType.DMA((len(STREAMS), 16)),
+            pltpu.SemaphoreType.DMA((groups,)),
+            pltpu.SemaphoreType.DMA((groups,)),
+            pltpu.SemaphoreType.DMA((groups,)),
+            pltpu.SemaphoreType.DMA((groups,)),
+            pltpu.SemaphoreType.DMA((RING * RING,)),
+            pltpu.SemaphoreType.DMA((vis // QBLK,)),
         ],
         compiler_params=pltpu.CompilerParams(collective_id=1, has_side_effects=True),
-        name="project_and_gather",
-    )(features, proj_weight, kv_weight)
-
-
-def backward_kernel(kvg_ref, w_ref, pre_ref, ft_ref, out_ref, *scratch):
+        name="fetch_project_gather",
+    )(
+        shard_owner.reshape(1, groups),
+        image_shard.reshape(1, images),
+        image_row.reshape(1, images),
+        feature_bank,
+        feature_scale,
+        proj_weight,
+        kv_weight,
+    )
+
+
+def attention(count_ref, doc_ref, kv_ref, q_ref, g_ref, kvg_ref, bias, dk, dv):
+    images, head = kv_ref.shape[0], kv_ref.shape[1] // 2
+    tokens = q_ref.shape[0]
+    chunk = min(tokens, 256)
+    f32, bf16 = jnp.float32, jnp.bfloat16
+    position = lax.broadcasted_iota(jnp.int32, (images, 1), 0)
+    image_doc = jnp.zeros((images, 1), jnp.int32)
+    end = 0
+    for d in range(count_ref.shape[1]):
+        end = end + count_ref[0, d]
+        image_doc = image_doc + (end <= position).astype(jnp.int32)
+    bias[...] = jnp.where(image_doc == doc_ref[...], 0.0, -1e30)
+    key_raw = kv_ref[:, :head]
+    values_low = kv_ref[:, head:].astype(bf16)
+    inv_norm = lax.rsqrt(jnp.mean(key_raw * key_raw, axis=-1, keepdims=True) + 1e-06)
+    key_unit = key_raw * inv_norm
+    key_low = key_unit.astype(bf16)
+    scale = head ** (-0.5)
+    dk[...] = jnp.zeros_like(dk)
+    dv[...] = jnp.zeros_like(dv)
+    across = (((1,), (1,)), ((), ()))
+
+    def one_head(h, _):
+        cols = pl.ds(pl.multiple_of(h * head, head), head)
+        for at in range(0, tokens, chunk):
+            query = q_ref[at : at + chunk, cols]
+            grad = g_ref[at : at + chunk, cols]
+            scores = lax.dot_general(key_low, query, across, preferred_element_type=f32) * scale
+            scores = scores + bias[:, at : at + chunk]
+            raised = jnp.exp(scores - jnp.max(scores, axis=0, keepdims=True))
+            probs = raised * (1.0 / jnp.sum(raised, axis=0, keepdims=True))
+            dprobs = lax.dot_general(values_low, grad, across, preferred_element_type=f32)
+            dscores = probs * (dprobs - jnp.sum(probs * dprobs, axis=0, keepdims=True))
+            dv[...] += jnp.dot(probs.astype(bf16), grad, preferred_element_type=f32)
+            dk[...] += jnp.dot(dscores.astype(bf16), query, preferred_element_type=f32)
+        return 0
+
+    lax.fori_loop(0, q_ref.shape[1] // head, one_head, 0)
+    key_grad = dk[...] * scale
+    raw_grad = inv_norm * (
+        key_grad - key_unit * jnp.mean(key_grad * key_unit, axis=-1, keepdims=True)
+    )
+    kvg_ref[:, :head] = raw_grad.astype(bf16)
+    kvg_ref[:, head:] = dv[...].astype(bf16)
+
+
+def backward_kernel(
+    count_ref, doc_ref, kv_ref, q_ref, g_ref, w_ref, pre_ref, ft_ref, out_ref, bias, kvg_ref, dk, dv, *scratch
+):
     images, width = pre_ref.shape
     half = width // 2
     rows, depth = out_ref.shape[0], ft_ref.shape[1]
@@ -189,6 +392,8 @@
     z_at = [lax.rem(z + dz, zs) for dz in range(zs)]
     z_peers = [dp_device(y, z_at[dz], core) for dz in range(1, zs)]
     ready = enter(ring_neighbours() + [core_peer, y_peer, both_peer] + z_peers)
+
+    attention(count_ref, doc_ref, kv_ref, q_ref, g_ref, kvg_ref, bias, dk, dv)
 
     def partial(ds, dx):
         block = w_ref[pl.ds(weight_rows(ds, dx, width), width), :]
@@ -329,7 +534,7 @@
         copy.wait_send()
 
 
-def backward(kv_grad, kv_weight, pre_act, feature_rows):
+def backward(image_count, text_doc, key_value, queries, out_grad, kv_weight, pre_act, feature_rows):
     images, width = pre_act.shape
     depth = feature_rows.shape[1]
     groups = lax.axis_size("dp")
@@ -348,9 +553,13 @@
     return pl.pallas_call(
         backward_kernel,
         out_shape=jax.ShapeDtypeStruct((rows, width), jnp.float32),
-        in_specs=[pl.BlockSpec(memory_space=pltpu.VMEM)] * 4,
+        in_specs=[pl.BlockSpec(memory_space=pltpu.SMEM)] + [pl.BlockSpec(memory_space=pltpu.VMEM)] * 7,
         out_specs=pl.BlockSpec(memory_space=pltpu.VMEM),
         scratch_shapes=[
+            pltpu.VMEM((images, text_doc.shape[1]), jnp.float32),
+            pltpu.VMEM((images, kv_weight.shape[1]), bf16),
+            pltpu.VMEM((images, kv_weight.shape[1] // 2), jnp.float32),
+            pltpu.VMEM((images, kv_weight.shape[1] // 2), jnp.float32),
             pltpu.VMEM((RING, RING, images, width), jnp.float32),
             pltpu.VMEM((depth, 4 * images), bf16),
             pltpu.VMEM((4 * images, width), bf16),
@@ -366,8 +575,8 @@
             pltpu.SemaphoreType.DMA((zs,)),
         ],
         compiler_params=pltpu.CompilerParams(collective_id=2, has_side_effects=True),
-        name="reduce_gradients",
-    )(kv_grad, kv_weight, pre_act, feature_rows)
+        name="attend_and_reduce",
+    )(image_count, text_doc, key_value, queries, out_grad, kv_weight, pre_act, feature_rows)
 
 
 def feature_rows_of(features):
@@ -376,55 +585,6 @@
     zs, rows = groups // 4, vis // groups
     tiles = features.T.reshape(2, zs, 2, rows, images)
     return jnp.moveaxis(tiles, 2, 1).reshape(4, zs * rows, images)
-
-
-def joined_along(tiles, dim):
-    tiles = jnp.moveaxis(tiles, 0, dim)
-    dims = tiles.shape
-    return tiles.reshape(*dims[:dim], dims[dim] * dims[dim + 1], *dims[dim + 2 :])
-
-
-def copy_for_each(array, axis):
-    peers = lax.axis_size(axis)
-    return lax.all_to_all(
-        jnp.broadcast_to(array[None], (peers, *array.shape)), axis, 0, 0, tiled=True
-    )
-
-
-def gathered_copies(array, axis, dim):
-    return joined_along(copy_for_each(array, axis), dim)
-
-
-def head_backward(query_heads, grad_heads, key_value, token_doc, image_doc):
-    head_size = key_value.shape[-1] // 2
-    key_raw = key_value[:, :head_size]
-    values_low = key_value[:, head_size:].astype(jnp.bfloat16)
-    inv_norm = lax.rsqrt(jnp.mean(key_raw * key_raw, axis=-1, keepdims=True) + 1e-06)
-    key_unit = key_raw * inv_norm
-    key_low = key_unit.astype(jnp.bfloat16)
-    score_scale = head_size ** (-0.5)
-    scores = (
-        jnp.einsum("tgd,id->gti", query_heads, key_low, preferred_element_type=jnp.float32)
-        * score_scale
-    )
-    same_doc = (token_doc[:, None] == image_doc[None, :])[None, :, :]
-    scores = jnp.where(same_doc, scores, -1e30)
-    row_max = jnp.max(scores, axis=-1, keepdims=True)
-    raised = jnp.where(same_doc, jnp.exp(scores - row_max), 0.0)
-    probs = raised / jnp.sum(raised, axis=-1, keepdims=True)
-    probs_low = probs.astype(jnp.bfloat16)
-    dprobs = jnp.einsum("tgd,id->gti", grad_heads, values_low, preferred_element_type=jnp.float32)
-    dscores = probs * (dprobs - jnp.sum(probs * dprobs, axis=-1, keepdims=True))
-    dscores_low = dscores.astype(jnp.bfloat16)
-    dvalues = jnp.einsum("gti,tgd->id", probs_low, grad_heads, preferred_element_type=jnp.float32)
-    key_grad = (
-        jnp.einsum("gti,tgd->id", dscores_low, query_heads, preferred_element_type=jnp.float32)
-        * score_scale
-    )
-    raw_grad = inv_norm * (
-        key_grad - key_unit * jnp.mean(key_grad * key_unit, axis=-1, keepdims=True)
-    )
-    return jnp.concatenate([raw_grad, dvalues], axis=-1).astype(jnp.bfloat16)
 
 
 def body(
@@ -440,39 +600,12 @@
     queries,
     out_grad,
 ):
-    groups = lax.axis_size("dp")
-    images = image_row.shape[0]
-    capacity = max(2, 2 * images // groups)
-    owner_dev = shard_owner[image_shard[:, 0]]
-    chosen = (owner_dev[:, None] == jnp.arange(groups, dtype=jnp.int32)[None, :]).astype(jnp.int32)
-    earlier = jnp.cumsum(chosen, axis=0) - chosen
-    slot_index = jnp.sum(earlier * chosen, axis=1)
-    wanted = (
-        jnp.zeros((groups * capacity,), jnp.int32)
-        .at[owner_dev * capacity + slot_index]
-        .set(image_row)
-    )
-    wanted = wanted.reshape(groups, capacity)
-    columns = jnp.repeat(feature_scale[0], QBLK)
-    slice_width = feature_bank.shape[1] // lax.axis_size(("section", "mp"))
-    first_column = lax.axis_index(("section", "mp")) * slice_width
-    stored = lax.dynamic_slice_in_dim(feature_bank, first_column, slice_width, 1)
-    factors = lax.dynamic_slice_in_dim(columns, first_column, slice_width, 0)
-    looked = stored[lax.all_to_all(wanted, "dp", split_axis=0, concat_axis=0, tiled=True)]
-    scaled = (looked.astype(jnp.float32) * factors).astype(jnp.bfloat16)
-    arrived = lax.all_to_all(scaled, "dp", split_axis=0, concat_axis=0, tiled=True)
-    features = arrived[owner_dev, slot_index]
-    features = gathered_copies(features, ("section", "mp"), 1)
-    pre_act, key_value = forward(features, proj_weight, kv_weight)
-    doc_ends = jnp.cumsum(image_count[0])
-    positions = jnp.arange(images, dtype=jnp.int32)
-    image_doc = jnp.sum((doc_ends[None, :] <= positions[:, None]).astype(jnp.int32), axis=1)
-    head_size = kv_weight.shape[1] // 2
-    tokens = queries.shape[0]
-    query_heads = queries.reshape(tokens, -1, head_size)
-    grad_heads = out_grad.reshape(tokens, -1, head_size)
-    kv_grad = head_backward(query_heads, grad_heads, key_value, text_doc[0], image_doc)
-    return backward(kv_grad, kv_weight, pre_act, feature_rows_of(features))
+    pre_act, key_value, features = forward(
+        shard_owner, image_shard, image_row, feature_bank, feature_scale, proj_weight, kv_weight
+    )
+    return backward(
+        image_count, text_doc, key_value, queries, out_grad, kv_weight, pre_act, feature_rows_of(features)
+    )
 
 
 def solution(mesh):

time: 167 us -> 145 us (0.87)
  Pallas kernels: 79.4 us -> 141 us
  starting transfers between devices: 26.5 us -> 0 us
  blocking collectives: 14.9 us -> 0 us
  local copies, waits for them, and re-layouts: 18.1 us -> 3.33 us
  waiting for transfers between devices: 13.5 us -> 0 us
  matrix products: 10.8 us -> 0 us
  other arithmetic: 3.4 us -> 0 us
    pallas_call x1, Pallas kernels: 28 us -> 80.7 us  [forward(): pl.pallas_call(forward_kernel, out_shape=(jax.ShapeDtypeStruct((images, w...]
    all_to_all x2 -> x0, starting transfers between devices: 26.5 us -> none  [the longest x1 18 us: body(): lax.all_to_all(wanted, 'dp', split_axis=0, concat_axis=0, tiled=True)]
    all_to_all x1 -> x0, blocking collectives: 14.9 us -> none  [body(): lax.all_to_all(scaled, 'dp', split_axis=0, concat_axis=0, tiled=True)]
    all_to_all x2 -> x0, waiting for transfers between devices: 13.5 us -> none  [the longest x1 9.43 us: body(): lax.all_to_all(wanted, 'dp', split_axis=0, concat_axis=0, tiled=True)]
    pallas_call x1, Pallas kernels: 51.4 us -> 60.5 us  [backward(): pl.pallas_call(backward_kernel, out_shape=jax.ShapeDtypeStruct((rows, wid...]
    reshape x4 -> x0, local copies, waits for them, and re-layouts: 8.16 us -> none  [the longest x1 3.95 us: body(): grad_heads = out_grad.reshape(tokens, -1, head_size)]
    dot_general x3 -> x0, matrix products: 5.85 us -> none  [the longest x1 3.72 us: head_backward(): jnp.einsum('gti,tgd->id', probs_low, grad_heads, preferred_element_type=j...]
    sub x1 -> x0, matrix products: 4.92 us -> none  [head_backward(): raised = jnp.where(same_doc, jnp.exp(scores - row_max), 0.0)]
  transfers between devices with their start and end apart: 2 -> 0, of which waited for: 2 -> 0; matrix products, arithmetic and copies ran while one was open for 5% -> 0% of each run, Pallas kernels for 0% -> 0%
where the time goes in v2:
time: 145 us
  Pallas kernels  141 us (97%)
  local copies, waits for them, and re-layouts  3.33 us (2%)
    pallas_call x1, Pallas kernels, forward(): pl.pallas_call(forward_kernel, out_shape=(jax.ShapeDtypeStruct((images, w...  80.7 us
    pallas_call x1, Pallas kernels, backward(): pl.pallas_call(backward_kernel, out_shape=jax.ShapeDtypeStruct((rows, wid...  60.5 us

profile of v2, /device:TPU:1, one launch (start us, length us, event | category | flops | bytes accessed | tf_op | source)
XLA Modules:
  0.0 144.5 jit_solution(7818822322920660648)
XLA Ops:
  0.0 80.7 %fetch_project_gather.1 = (f32[128,512]{1,0:T(8,128)}, f32[128,256]{1,0:T(8,128)}, bf16[128,1152]{1,0:T(8,128)(2,1)}) custom-call(s32[1,48]{1,0:T(1,128)} %bitcast.11, s32[1,128]{1,0:T(1,128)} %bitcast.12, s32[1,128]{1,0:T(1,128)} %bitcast.13, bf16[256,1152]{1,0:T(8,128)(2,1)} %bank_ref.1, f32[1,9]{1,0:T(1,128)} %scale_ref.1, bf16[1152,512]{1,0:T(8,128)(2,1)} %proj_ref.1, ...), custom_call_target="tpu_custom_call" | custom-call | tf_op jit(solution)/shard_map/fetch_project_gather/pallas_call | solution.py:283
  80.7 1.2 copy.13
  81.9 0.7 copy.14
  82.6 60.5 %attend_and_reduce.1 = f32[24,512]{1,0:T(8,128)} custom-call(s32[1,8]{1,0:T(1,128)} %count_ref.1, s32[1,1024]{1,0:T(1,128)} %doc_ref.1, f32[128,256]{1,0:T(8,128)} %get-tuple-element.8.kv_ref, bf16[1024,1024]{1,0:T(8,128)(2,1)} %q_ref.1, bf16[1024,1024]{1,0:T(8,128)(2,1)} %g_ref.1, bf16[8192,256]{1,0:T(8,128)(2,1)} %w_ref.3, ...), custom_call_target="tpu_custom_call" | custom-call | tf_op jit(solution)/shard_map/attend_and_reduce/pallas_call | solution.py:553
  143.1 1.4 copy.16

commit v3 on v2

--- a/solution.py
+++ b/solution.py
@@ -1,5 +1,3 @@
-import functools
-
 import jax
 import jax.numpy as jnp
 from jax import lax
@@ -9,7 +7,8 @@
 
 QBLK = 128
 RING = 4
-STREAMS = ((0, 3, "x"), (3, 6, "x"), (6, 8, "y"))
+SUM_STREAMS = tuple((n, n + 1, "x") for n in range(6)) + ((6, 7, "y"), (7, 8, "y"))
+GATHER_STREAMS = ((0, 2, "y"), (2, 4, "y"), (4, 6, "y"), (6, 8, "x"))
 AXIS = {"x": "mp", "y": "section"}
 
 
@@ -35,13 +34,6 @@
     s = lax.rem(lax.axis_index("section") + ds, RING)
     m = lax.rem(lax.axis_index("mp") + dx, RING)
     return pl.multiple_of((s * RING + m) * width, width)
-
-
-def enter(targets):
-    barrier = pltpu.get_barrier_semaphore()
-    for target in targets:
-        pl.semaphore_signal(barrier, 1, device_id=target, device_id_type=pl.DeviceIdType.MESH)
-    return lambda: pl.semaphore_wait(barrier, len(targets))
 
 
 def remote(src, dst, send_sem, recv_sem, target):
@@ -55,24 +47,35 @@
     )
 
 
-def ring_neighbours():
-    return [ring_target(a, d) for a in "xy" for d in (1, -1)]
-
-
-def forward_kernel(
-    owner_ref, shard_ref, row_ref, bank_ref, scale_ref, proj_ref, w_ref,
-    pre_ref, kv_ref, feat_ref,
+def step_kernel(
+    owner_ref, shard_ref, row_ref, scale_ref, count_ref, doc_ref,
+    bank_hbm, proj_hbm, w_hbm, q_hbm, g_hbm,
+    out_ref,
+    bank_ref, proj_ref, w_ref, q_ref, g_ref, pre_ref, kv_ref, load_sem,
     gat, wsend, wrecv, spread, rsend, rrecv, fgat,
     send_sem, recv_sem, wsend_sem, wrecv_sem, rsend_sem, rrecv_sem, fsend_sem, frecv_sem,
+    *scratch,
 ):
+    loads = [
+        pltpu.make_async_copy(src, dst, load_sem.at[n])
+        for n, (src, dst) in enumerate(
+            ((bank_hbm, bank_ref), (proj_hbm, proj_ref), (w_hbm, w_ref), (q_hbm, q_ref), (g_hbm, g_ref))
+        )
+    ]
     images, width = pre_ref.shape
     half = width // 2
     groups, slots = rsend.shape[:2]
     bank = bank_ref.shape[0]
     blocks = fgat.shape[0]
     here = lax.axis_index("dp")
-    member = lax.axis_index("section") * RING + lax.axis_index("mp")
-    block_at = lax.rem(member, blocks)
+    at_s, at_m = lax.axis_index("section"), lax.axis_index("mp")
+    is_extra = jnp.logical_and(at_s == 0, at_m == 1)
+    holds = jnp.logical_or(lax.rem(at_s + at_m, 2) == 0, is_extra)
+    block_at = jnp.where(is_extra, 2 * RING, 2 * at_s + at_m // 2)
+
+    def holder(b):
+        return (0, 1) if b == 2 * RING else (b // 2, 2 * (b % 2) + (b // 2) % 2)
+
     f32, bf16 = jnp.float32, jnp.bfloat16
 
     def dp_peer(step):
@@ -92,6 +95,8 @@
     lax.fori_loop(1, groups, greet, 0)
     for ds, dx in others:
         pl.semaphore_signal(barrier, 1, device_id=other(ds, dx), device_id_type=pl.DeviceIdType.MESH)
+    for load in loads:
+        load.start()
 
     def iota(shape, dim):
         return lax.broadcasted_iota(jnp.int32, shape, dim)
@@ -152,6 +157,7 @@
     own_slot = lax.rem(iota((entries, QBLK), 0), slots) == iota((entries, QBLK), 1)
     row = jnp.sum(jnp.where(own_slot, spread[...], 0.0), axis=1, keepdims=True)
     picks = (row == iota((entries, bank), 1).astype(f32)).astype(bf16)
+    loads[0].wait()
     columns = pl.ds(pl.multiple_of(block_at * QBLK, QBLK), QBLK)
     looked = jnp.dot(picks, bank_ref[:, columns], preferred_element_type=f32)
     scaled = looked * scale_ref[0, block_at]
@@ -163,7 +169,7 @@
             fgat.at[block_at], fgat.at[block_at], fsend_sem.at[n], frecv_sem.at[block_at], other(ds, dx)
         )
 
-    @pl.when(member < blocks)
+    @pl.when(holds)
     def _():
         every_step(lambda step: answer(step).start())
         rrecv[0] = rsend[0]
@@ -178,15 +184,20 @@
             block_copy(ds, dx).start()
 
     pre = jnp.zeros((images, width), f32)
+    loads[1].wait()
+    same = (iota((QBLK, QBLK), 0) == iota((QBLK, QBLK), 1)).astype(bf16)
+    across = (((1,), (1,)), ((), ()))
+    feat_t = scratch[0]
     for b in range(blocks):
-        @pl.when(member != b)
+        hs, hm = holder(b)
+
+        @pl.when(jnp.logical_or(at_s != hs, at_m != hm))
         def _():
             remote(
                 fgat.at[b], fgat.at[b], fsend_sem.at[0], frecv_sem.at[b], other(0, 1)
             ).wait_recv()
 
         values = fgat[b]
-        feat_ref[:, b * QBLK : (b + 1) * QBLK] = values
         pre = pre + jnp.dot(values, proj_ref[b * QBLK : (b + 1) * QBLK, :], preferred_element_type=f32)
     pre_ref[...] = pre
     gat[0, 0] = gelu(pre).astype(bf16)
@@ -210,8 +221,8 @@
         return gat.at[a, b, lo:hi, cols]
 
     unit = images // 8
-    streams = [(a * unit, b * unit, "y" if f == "x" else "x") for a, b, f in STREAMS]
-    order = (2, 0, 1)
+    streams = [(a * unit, b * unit, f) for a, b, f in GATHER_STREAMS]
+    order = (3, 0, 1, 2)
 
     def second(c, i):
         lo, hi, first = streams[c]
@@ -253,70 +264,39 @@
         rows = pl.ds(weight_rows(ds, dx, width), width)
         return jnp.dot(gat[ds, dx], w_ref[rows, :], preferred_element_type=jnp.float32)
 
+    for b in range(blocks):
+        feat_t[b * QBLK : (b + 1) * QBLK, :] = lax.dot_general(
+            same, fgat[b], across, preferred_element_type=f32
+        ).astype(bf16)
+    loads[2].wait()
     kv = term(0, 0)
     waited = {("p", 0, 0), ("p", 3, 1), ("p", 1, 0), ("p", 2, 1), ("a", 0), ("a", 1), ("b", 0), ("b", 1)}
+    near = [(ds, dx) for ds in (0, 1, 3) for dx in (0, 1, 3)]
     for (c, key), copy in copies.items():
-        if key not in waited:
+        if key[0] == "p" and key not in waited:
+            copy.wait_recv()
+    for ds, dx in near[1:]:
+        kv = kv + term(ds, dx)
+    for (c, key), copy in copies.items():
+        if key[0] == "q":
             copy.wait_recv()
     for ds in range(RING):
         for dx in range(RING):
-            if (ds, dx) != (0, 0):
+            if (ds, dx) not in near:
                 kv = kv + term(ds, dx)
     kv_ref[...] = kv
+    loads[3].wait()
+    loads[4].wait()
+    reduce_part(count_ref, doc_ref, kv_ref, q_ref, g_ref, w_ref, pre_ref, out_ref, *scratch)
     for copy in started:
         copy.wait_send()
     every_step(lambda step: request(step).wait_send())
 
-    @pl.when(member < blocks)
+    @pl.when(holds)
     def _():
         every_step(lambda step: answer(step).wait_send())
         for ds, dx in others:
             block_copy(ds, dx).wait_send()
-
-
-def forward(shard_owner, image_shard, image_row, feature_bank, feature_scale, proj_weight, kv_weight):
-    images, width = image_row.shape[0], proj_weight.shape[1]
-    groups, vis = shard_owner.shape[0], proj_weight.shape[0]
-    slots = 8
-    f32, bf16 = jnp.float32, jnp.bfloat16
-    vmem = pl.BlockSpec(memory_space=pltpu.VMEM)
-    return pl.pallas_call(
-        forward_kernel,
-        out_shape=(
-            jax.ShapeDtypeStruct((images, width), f32),
-            jax.ShapeDtypeStruct((images, kv_weight.shape[1]), f32),
-            jax.ShapeDtypeStruct((images, vis), bf16),
-        ),
-        in_specs=[vmem] * 4 + [pl.BlockSpec(memory_space=pltpu.SMEM)] + [vmem] * 2,
-        out_specs=(vmem,) * 3,
-        scratch_shapes=[
-            pltpu.VMEM((RING, RING, images, width), bf16),
-            pltpu.VMEM((groups, 1, QBLK), f32),
-            pltpu.VMEM((groups, 1, QBLK), f32),
-            pltpu.VMEM((groups * slots, QBLK), f32),
-            pltpu.VMEM((groups, slots, QBLK), bf16),
-            pltpu.VMEM((groups, slots, QBLK), bf16),
-            pltpu.VMEM((vis // QBLK, images, QBLK), bf16),
-            pltpu.SemaphoreType.DMA((len(STREAMS), 16)),
-            pltpu.SemaphoreType.DMA((len(STREAMS), 16)),
-            pltpu.SemaphoreType.DMA((groups,)),
-            pltpu.SemaphoreType.DMA((groups,)),
-            pltpu.SemaphoreType.DMA((groups,)),
-            pltpu.SemaphoreType.DMA((groups,)),
-            pltpu.SemaphoreType.DMA((RING * RING,)),
-            pltpu.SemaphoreType.DMA((vis // QBLK,)),
-        ],
-        compiler_params=pltpu.CompilerParams(collective_id=1, has_side_effects=True),
-        name="fetch_project_gather",
-    )(
-        shard_owner.reshape(1, groups),
-        image_shard.reshape(1, images),
-        image_row.reshape(1, images),
-        feature_bank,
-        feature_scale,
-        proj_weight,
-        kv_weight,
-    )
 
 
 def attention(count_ref, doc_ref, kv_ref, q_ref, g_ref, kvg_ref, bias, dk, dv):
@@ -365,18 +345,18 @@
     kvg_ref[:, head:] = dv[...].astype(bf16)
 
 
-def backward_kernel(
-    count_ref, doc_ref, kv_ref, q_ref, g_ref, w_ref, pre_ref, ft_ref, out_ref, bias, kvg_ref, dk, dv, *scratch
+def reduce_part(
+    count_ref, doc_ref, kv_ref, q_ref, g_ref, w_ref, pre_ref, out_ref, feat_t, bias, kvg_ref, dk, dv, *scratch
 ):
     images, width = pre_ref.shape
     half = width // 2
-    rows, depth = out_ref.shape[0], ft_ref.shape[1]
-    zs = depth // rows
+    rows, depth = out_ref.shape[0], feat_t.shape[0] // 2
+    zs = depth // (2 * rows)
     part, feat, pgs, sums, zsend, zrecv = scratch[:6]
-    bufs = [scratch[6 + 8 * c : 14 + 8 * c] for c in range(len(STREAMS))]
-    send_sem, recv_sem, dsend_sem, drecv_sem, zsend_sem, zrecv_sem = scratch[6 + 8 * len(STREAMS) :]
+    bufs = [scratch[6 + 8 * c : 14 + 8 * c] for c in range(len(SUM_STREAMS))]
+    send_sem, recv_sem, dsend_sem, drecv_sem, zsend_sem, zrecv_sem = scratch[6 + 8 * len(SUM_STREAMS) :]
     unit = images // 8
-    streams = [(a * unit, b * unit, f) for a, b, f in STREAMS]
+    streams = [(a * unit, b * unit, f) for a, b, f in SUM_STREAMS]
 
     place = lax.axis_index("dp")
     core = lax.rem(place, 2)
@@ -388,12 +368,8 @@
 
     core_peer = dp_device(y, z, 1 - core)
     y_peer = dp_device(1 - y, z, core)
-    both_peer = dp_device(1 - y, z, 1 - core)
     z_at = [lax.rem(z + dz, zs) for dz in range(zs)]
     z_peers = [dp_device(y, z_at[dz], core) for dz in range(1, zs)]
-    ready = enter(ring_neighbours() + [core_peer, y_peer, both_peer] + z_peers)
-
-    attention(count_ref, doc_ref, kv_ref, q_ref, g_ref, kvg_ref, bias, dk, dv)
 
     def partial(ds, dx):
         block = w_ref[pl.ds(weight_rows(ds, dx, width), width), :]
@@ -401,9 +377,6 @@
             kvg_ref[...], block, (((1,), (1,)), ((), ())), preferred_element_type=jnp.float32
         )
 
-    early = [(2, 2)] + [(ds, 2) for ds in (0, 1, 3)] + [(2, dx) for dx in (0, 1, 3)]
-    for ds, dx in early:
-        partial(ds, dx)
     copies = {}
     started = []
 
@@ -487,33 +460,53 @@
         copies["dp", c, 0].wait_recv()
         dp_send(c, 2, pg_rows(c, 2), pg_rows(c, 3), core_peer)
 
-    ready()
-    for c in (2, 0, 1):
+    last = len(SUM_STREAMS)
+
+    def y_rows(yy):
+        return feat_t.at[pl.ds(pl.multiple_of(yy * depth, depth), depth), :]
+
+    def slot_of(k):
+        return feat.at[:, k * images : (k + 1) * images]
+
+    dp_send(last, 0, y_rows(1 - y), slot_of(2), y_peer)
+    dp_send(last, 1, y_rows(y), slot_of(1), core_peer)
+    slot_of(0)[...] = y_rows(y)[...]
+    attention(count_ref, doc_ref, kv_ref, q_ref, g_ref, kvg_ref, bias, dk, dv)
+    wide = [c for c in range(last) if streams[c][2] == "x"]
+    tall = [c for c in range(last) if streams[c][2] == "y"]
+    for ds in (2, 0, 1, 3):
+        partial(ds, 2)
+    for c in wide:
         step1(c)
-    last = len(STREAMS)
-    for k, (yy, cc, target) in enumerate(
-        ((y, 1 - core, core_peer), (1 - y, core, y_peer), (1 - y, 1 - core, both_peer))
-    ):
-        dp_send(
-            last, k, ft_ref.at[yy * 2 + cc], feat.at[:, (k + 1) * images : (k + 2) * images], target
-        )
-    for ds in range(RING):
-        for dx in range(RING):
-            if (ds, dx) not in early:
-                partial(ds, dx)
-    feat[:, 0:images] = ft_ref[y * 2 + core]
-    step2(0), step2(2), step2(1)
-    step3(0), step3(2), step4(0), step4(2), step3(1), finish(2), finish(0), step4(1)
-    relay(2), relay(0), finish(1), relay(1)
+    for dx in (0, 1, 3):
+        partial(2, dx)
+    for c in tall:
+        step1(c)
+    for dx in (1, 3, 0):
+        for ds in (0, 1, 3):
+            partial(ds, dx)
+    tasks = []
+    for n, c in enumerate(wide):
+        third = 6 + 1.4 * (n + 1)
+        times = (2.5 + 0.7 * n, third, third + 3, third + 6, third + 8.2)
+        tasks += [(t, k, c) for k, t in enumerate(times)]
+    for n, c in enumerate(tall):
+        third = 8 + 2.8 * (n + 1)
+        times = (4 + 1.4 * n, third, third + 2.5, third + 5, third + 7.2)
+        tasks += [(t, k, c) for k, t in enumerate(times)]
+    for _, k, c in sorted(tasks):
+        (step2, step3, step4, finish, relay)[k](c)
+    copies["dp", last, 0].wait_recv()
+    dp_send(last, 2, slot_of(2), slot_of(3), core_peer)
     for c in range(last):
         copies["dp", c, 1].wait_recv()
         copies["dp", c, 2].wait_recv()
-    for k in range(3):
+    for k in (1, 2):
         copies["dp", last, k].wait_recv()
     sums[...] = jnp.dot(feat[...], pgs[...], preferred_element_type=jnp.float32)
 
     def folded(dz):
-        value = sums[pl.ds(pl.multiple_of(z_at[dz] * rows, rows), rows), :]
+        value = sums[pl.ds(pl.multiple_of((2 * z_at[dz] + core) * rows, rows), rows), :]
         return jnp.concatenate([value[:, :half], value[:, half:]], axis=0)
 
     zcopies = []
@@ -534,59 +527,6 @@
         copy.wait_send()
 
 
-def backward(image_count, text_doc, key_value, queries, out_grad, kv_weight, pre_act, feature_rows):
-    images, width = pre_act.shape
-    depth = feature_rows.shape[1]
-    groups = lax.axis_size("dp")
-    rows = 4 * depth // groups
-    zs = depth // rows
-    half = width // 2
-    unit = images // 8
-    bf16 = jnp.bfloat16
-    ring_bufs = []
-    for a, b, _ in STREAMS:
-        n = (b - a) * unit
-        ring_bufs += [pltpu.VMEM((2, 2, n, width), bf16)] * 2
-        ring_bufs += [pltpu.VMEM((2, RING, n, width), bf16)] * 2
-        ring_bufs += [pltpu.VMEM((2, n, half), bf16)] * 2
-        ring_bufs += [pltpu.VMEM((2, n, width), bf16)] * 2
-    return pl.pallas_call(
-        backward_kernel,
-        out_shape=jax.ShapeDtypeStruct((rows, width), jnp.float32),
-        in_specs=[pl.BlockSpec(memory_space=pltpu.SMEM)] + [pl.BlockSpec(memory_space=pltpu.VMEM)] * 7,
-        out_specs=pl.BlockSpec(memory_space=pltpu.VMEM),
-        scratch_shapes=[
-            pltpu.VMEM((images, text_doc.shape[1]), jnp.float32),
-            pltpu.VMEM((images, kv_weight.shape[1]), bf16),
-            pltpu.VMEM((images, kv_weight.shape[1] // 2), jnp.float32),
-            pltpu.VMEM((images, kv_weight.shape[1] // 2), jnp.float32),
-            pltpu.VMEM((RING, RING, images, width), jnp.float32),
-            pltpu.VMEM((depth, 4 * images), bf16),
-            pltpu.VMEM((4 * images, width), bf16),
-            pltpu.VMEM((depth, width), jnp.float32),
-            pltpu.VMEM((zs, 2 * rows, half), bf16),
-            pltpu.VMEM((zs, 2 * rows, half), bf16),
-            *ring_bufs,
-            pltpu.SemaphoreType.DMA((len(STREAMS), 8)),
-            pltpu.SemaphoreType.DMA((len(STREAMS), 8)),
-            pltpu.SemaphoreType.DMA((len(STREAMS) + 1, 3)),
-            pltpu.SemaphoreType.DMA((len(STREAMS) + 1, 3)),
-            pltpu.SemaphoreType.DMA((zs,)),
-            pltpu.SemaphoreType.DMA((zs,)),
-        ],
-        compiler_params=pltpu.CompilerParams(collective_id=2, has_side_effects=True),
-        name="attend_and_reduce",
-    )(image_count, text_doc, key_value, queries, out_grad, kv_weight, pre_act, feature_rows)
-
-
-def feature_rows_of(features):
-    images, vis = features.shape
-    groups = lax.axis_size("dp")
-    zs, rows = groups // 4, vis // groups
-    tiles = features.T.reshape(2, zs, 2, rows, images)
-    return jnp.moveaxis(tiles, 2, 1).reshape(4, zs * rows, images)
-
-
 def body(
     feature_bank,
     feature_scale,
@@ -600,11 +540,68 @@
     queries,
     out_grad,
 ):
-    pre_act, key_value, features = forward(
-        shard_owner, image_shard, image_row, feature_bank, feature_scale, proj_weight, kv_weight
-    )
-    return backward(
-        image_count, text_doc, key_value, queries, out_grad, kv_weight, pre_act, feature_rows_of(features)
+    images, (vis, width) = image_row.shape[0], proj_weight.shape
+    groups, features = shard_owner.shape[0], kv_weight.shape[1]
+    rows = vis // groups
+    zs, half, unit, slots = groups // 4, width // 2, images // 8, 8
+    f32, bf16 = jnp.float32, jnp.bfloat16
+    vmem, smem, hbm = (
+        pl.BlockSpec(memory_space=space) for space in (pltpu.VMEM, pltpu.SMEM, pl.ANY)
+    )
+    dma = pltpu.SemaphoreType.DMA
+    ring_bufs = []
+    for a, b, _ in SUM_STREAMS:
+        n = (b - a) * unit
+        ring_bufs += [pltpu.VMEM((2, 2, n, width), bf16)] * 2
+        ring_bufs += [pltpu.VMEM((2, RING, n, width), bf16)] * 2
+        ring_bufs += [pltpu.VMEM((2, n, half), bf16)] * 2
+        ring_bufs += [pltpu.VMEM((2, n, width), bf16)] * 2
+    large = (feature_bank, proj_weight, kv_weight, queries, out_grad)
+    return pl.pallas_call(
+        step_kernel,
+        out_shape=jax.ShapeDtypeStruct((rows, width), f32),
+        in_specs=[vmem] * 3 + [smem] * 2 + [vmem] + [hbm] * 5,
+        out_specs=vmem,
+        scratch_shapes=[
+            *[pltpu.VMEM(array.shape, array.dtype) for array in large],
+            pltpu.VMEM((images, width), f32),
+            pltpu.VMEM((images, features), f32),
+            dma((len(large),)),
+            pltpu.VMEM((RING, RING, images, width), bf16),
+            pltpu.VMEM((groups, 1, QBLK), f32),
+            pltpu.VMEM((groups, 1, QBLK), f32),
+            pltpu.VMEM((groups * slots, QBLK), f32),
+            pltpu.VMEM((groups, slots, QBLK), bf16),
+            pltpu.VMEM((groups, slots, QBLK), bf16),
+            pltpu.VMEM((vis // QBLK, images, QBLK), bf16),
+            *[dma((len(GATHER_STREAMS), 16))] * 2,
+            *[dma((groups,))] * 4,
+            dma((RING * RING,)),
+            dma((vis // QBLK,)),
+            pltpu.VMEM((vis, images), bf16),
+            pltpu.VMEM((images, text_doc.shape[1]), f32),
+            pltpu.VMEM((images, features), bf16),
+            *[pltpu.VMEM((images, features // 2), f32)] * 2,
+            pltpu.VMEM((RING, RING, images, width), f32),
+            pltpu.VMEM((vis // 2, 4 * images), bf16),
+            pltpu.VMEM((4 * images, width), bf16),
+            pltpu.VMEM((vis // 2, width), f32),
+            *[pltpu.VMEM((zs, 2 * rows, half), bf16)] * 2,
+            *ring_bufs,
+            *[dma((len(SUM_STREAMS), 8))] * 2,
+            *[dma((len(SUM_STREAMS) + 1, 3))] * 2,
+            *[dma((zs,))] * 2,
+        ],
+        compiler_params=pltpu.CompilerParams(collective_id=1, has_side_effects=True),
+        name="projector_step",
+    )(
+        shard_owner.reshape(1, groups),
+        image_shard.reshape(1, images),
+        image_row.reshape(1, images),
+        feature_scale,
+        image_count,
+        text_doc,
+        *large,
     )
 
 

time: 145 us -> 133 us (0.917)
  Pallas kernels: 141 us -> 132 us
  local copies, waits for them, and re-layouts: 3.33 us -> 1.42 us
    pallas_call x2 -> x1, Pallas kernels: 141 us -> 132 us  [body(): pl.pallas_call(step_kernel, out_shape=jax.ShapeDtypeStruct((rows, width),...]
    transpose x2 -> x0, local copies, waits for them, and re-layouts: 1.91 us -> none  [the longest x1 1.17 us: feature_rows_of(): tiles = features.T.reshape(2, zs, 2, rows, images)]
where the time goes in v3:
time: 133 us
  Pallas kernels  132 us (99%)
  local copies, waits for them, and re-layouts  1.42 us (1%)
    pallas_call x1, Pallas kernels, body(): pl.pallas_call(step_kernel, out_shape=jax.ShapeDtypeStruct((rows, width),...  132 us

profile of v3, /device:TPU:1, one launch (start us, length us, event | category | flops | bytes accessed | tf_op | source)
XLA Modules:
  0.0 133.0 jit_solution(604696217355176678)
XLA Ops:
  0.0 131.6 %projector_step.1 = f32[24,512]{1,0:T(8,128)} custom-call(s32[1,48]{1,0:T(1,128)} %bitcast.3, s32[1,128]{1,0:T(1,128)} %bitcast.4, s32[1,128]{1,0:T(1,128)} %bitcast.5, f32[1,9]{1,0:T(1,128)} %scale_ref.1, s32[1,8]{1,0:T(1,128)} %count_ref.1, s32[1,1024]{1,0:T(1,128)} %doc_ref.1, bf16[256,1152]{1,0:T(8,128)(2,1)} %bank_hbm.1, bf16[1152,512]{1,0:T(8,128)(2,1)} %proj_hbm.1, ...), custom_call_target="tpu_custom_call" | custom-call | tf_op jit(solution)/shard_map/projector_step/pallas_call | solution.py:560
  131.6 1.4 %copy.13 = f32[24,512]{1,0:T(8,128)} copy(f32[24,512]{1,0:T(8,128)} %projector_step.1) | data formatting | bytes 98304

commit v4 on v3

--- a/solution.py
+++ b/solution.py
@@ -88,11 +88,10 @@
 
     barrier = pltpu.get_barrier_semaphore()
 
-    def greet(step, _):
+    zs = groups // 4
+    far_first = sorted(range(1, groups), key=lambda n: -min(n // 2 % zs, zs - n // 2 % zs))
+    for step in far_first:
         pl.semaphore_signal(barrier, 1, device_id=dp_peer(step), device_id_type=pl.DeviceIdType.MESH)
-        return 0
-
-    lax.fori_loop(1, groups, greet, 0)
     for ds, dx in others:
         pl.semaphore_signal(barrier, 1, device_id=other(ds, dx), device_id_type=pl.DeviceIdType.MESH)
     for load in loads:
@@ -133,17 +132,14 @@
             rsend.at[step], rrecv.at[step], rsend_sem.at[step], rrecv_sem.at[step], dp_peer(groups - step)
         )
 
-    def every_step(do):
-        def run(step, _):
+    def every_step(do, order=far_first[::-1]):
+        for step in order:
             do(step)
-            return 0
-
-        lax.fori_loop(1, groups, run, 0)
-
-    every_step(lambda step: request(step).start())
+
+    every_step(lambda step: request(step).start(), far_first)
 
     def expand(step, row):
-        spread[pl.ds(pl.multiple_of(step * slots, slots), slots), :] = jnp.broadcast_to(row, (slots, QBLK))
+        spread[step * slots : (step + 1) * slots, :] = jnp.broadcast_to(row, (slots, QBLK))
 
     expand(0, wsend[0])
 
@@ -171,7 +167,7 @@
 
     @pl.when(holds)
     def _():
-        every_step(lambda step: answer(step).start())
+        every_step(lambda step: answer(step).start(), far_first)
         rrecv[0] = rsend[0]
         at = iota((entries, images), 0)
         selected = (at == ahead * slots + slot).astype(bf16)
@@ -302,7 +298,7 @@
 def attention(count_ref, doc_ref, kv_ref, q_ref, g_ref, kvg_ref, bias, dk, dv):
     images, head = kv_ref.shape[0], kv_ref.shape[1] // 2
     tokens = q_ref.shape[0]
-    chunk = min(tokens, 256)
+    chunk = min(tokens, 1024)
     f32, bf16 = jnp.float32, jnp.bfloat16
     position = lax.broadcasted_iota(jnp.int32, (images, 1), 0)
     image_doc = jnp.zeros((images, 1), jnp.int32)
@@ -336,7 +332,7 @@
             dk[...] += jnp.dot(dscores.astype(bf16), query, preferred_element_type=f32)
         return 0
 
-    lax.fori_loop(0, q_ref.shape[1] // head, one_head, 0)
+    lax.fori_loop(0, q_ref.shape[1] // head, one_head, 0, unroll=2)
     key_grad = dk[...] * scale
     raw_grad = inv_norm * (
         key_grad - key_unit * jnp.mean(key_grad * key_unit, axis=-1, keepdims=True)

time: 133 us -> 126 us (0.947)
  Pallas kernels: 132 us -> 124 us
    pallas_call x1, Pallas kernels: 132 us -> 124 us  [body(): pl.pallas_call(step_kernel, out_shape=jax.ShapeDtypeStruct((rows, width),...]
where the time goes in v4:
time: 126 us
  Pallas kernels  124 us (98%)
  local copies, waits for them, and re-layouts  1.42 us (1%)
    pallas_call x1, Pallas kernels, body(): pl.pallas_call(step_kernel, out_shape=jax.ShapeDtypeStruct((rows, width),...  124 us

profile of v4, /device:TPU:1, one launch (start us, length us, event | category | flops | bytes accessed | tf_op | source)
XLA Modules:
  0.0 125.7 jit_solution(17915386582909832617)
XLA Ops:
  0.0 124.3 %projector_step.1 = f32[24,512]{1,0:T(8,128)} custom-call(s32[1,48]{1,0:T(1,128)} %bitcast.3, s32[1,128]{1,0:T(1,128)} %bitcast.4, s32[1,128]{1,0:T(1,128)} %bitcast.5, f32[1,9]{1,0:T(1,128)} %scale_ref.1, s32[1,8]{1,0:T(1,128)} %count_ref.1, s32[1,1024]{1,0:T(1,128)} %doc_ref.1, bf16[256,1152]{1,0:T(8,128)(2,1)} %bank_hbm.1, bf16[1152,512]{1,0:T(8,128)(2,1)} %proj_hbm.1, ...), custom_call_target="tpu_custom_call" | custom-call | tf_op jit(solution)/shard_map/projector_step/pallas_call | solution.py:556
  124.3 1.4 %copy.13 = f32[24,512]{1,0:T(8,128)} copy(f32[24,512]{1,0:T(8,128)} %projector_step.1) | data formatting | bytes 98304
